TPU v7x, 256 devices: a whole 4x4x8 slice. The times are simulated.
256 devices in a mesh: group: 8 (over y, core), dev: 32 (over z, x).
Axes of the slice: x: 4, y: 4, z: 8, core: 2. Of those that a mesh axis runs over, the one named last changes fastest.
Arguments:
- points: float32 [440, 131072], P(None, ('group', 'dev')), may hold values from -6 to 6
- residual: float32 [147, 131072], P(None, ('group', 'dev')), may hold values from -6 to 6
- coeffs: float32 [147, 131072], P(None, ('group', 'dev')), may hold values from -3 to 3
- owners: int32 [2], replicated, may hold values from 0 to 255
- offsets: int32 [2], replicated, may hold values from 0 to 256
Outputs:
- new_residual: float32 [147, 131072], P(None, ('group', 'dev'))
- new_coeffs: float32 [147, 131072], P(None, ('group', 'dev'))
All inputs are finite; a program needn't handle non-finite values.
Results may differ from a plain program's by a relative error of at most 0.0003.
Values sent between devices are 32-bit elements; how exact they have to be, the bound alone decides.
No kernel may reach another device: no remote copies, remote signals or barrier semaphores. Data moves between devices by JAX's collectives and lax.ppermute only.
A program may use at most 64 MiB of HBM per device.

v0:
```python
import jax
import jax.numpy as jnp
from jax import lax
from jax.sharding import PartitionSpec as P

BLOCK = 256


ridge = 2.0
step_norm = 1.5


def spread_2(value, axis, root):
    mine = lax.axis_index(axis) == root
    return lax.psum(jnp.where(mine, value, jnp.zeros_like(value)), axis)


def kernel_tile(cols, block):
    cross = lax.dot_general(
        block,
        cols,
        (((0,), (0,)), ((), ())),
        precision=lax.Precision.HIGHEST,
        preferred_element_type=jnp.float32,
    )
    dist = (
        jnp.sum(block * block, axis=0)[:, None]
        + jnp.sum(cols * cols, axis=0)[None, :]
        - 2.0 * cross
    )
    return jnp.exp(-dist / cols.shape[0])


def precondition(grad, block):
    gram = kernel_tile(block, block) + ridge * jnp.eye(block.shape[1], dtype=jnp.float32)
    lower = jnp.linalg.cholesky(gram)
    inner = lax.linalg.triangular_solve(lower, grad.T, left_side=True, lower=True)
    solved = lax.linalg.triangular_solve(lower, inner, left_side=True, lower=True, transpose_a=True)
    scale = step_norm / jnp.sqrt(jnp.mean(grad * grad) + 1e-06)
    return scale * solved.T


def contract(left, right):
    return lax.dot_general(
        left,
        right,
        (((1,), (1,)), ((), ())),
        precision=lax.Precision.HIGHEST,
        preferred_element_type=jnp.float32,
    )


def spread(delta, tile):
    return jnp.dot(delta, tile, precision=lax.Precision.HIGHEST, preferred_element_type=jnp.float32)


def body(points, residual, coeffs, owners, offsets):
    here = lax.axis_index(("group", "dev"))
    for step in range(2):
        local = lax.dynamic_slice_in_dim(points, offsets[step], BLOCK, 1)
        block = spread_2(local, ("group", "dev"), owners[step])
        tile = kernel_tile(points, block)
        grad = lax.psum(contract(residual, tile), ("group", "dev"))
        delta = precondition(grad, block)
        residual = residual - spread(delta, tile)
        current = lax.dynamic_slice_in_dim(coeffs, offsets[step], BLOCK, 1)
        mine = jnp.where(here == owners[step], delta, jnp.zeros_like(delta))
        coeffs = lax.dynamic_update_slice_in_dim(coeffs, current + mine, offsets[step], 1)
    return (residual, coeffs)


def solution(mesh):
    return jax.shard_map(
        body,
        mesh=mesh,
        in_specs=(
            P(None, ("group", "dev")),
            P(None, ("group", "dev")),
            P(None, ("group", "dev")),
            P(),
            P(),
        ),
        out_specs=(P(None, ("group", "dev")), P(None, ("group", "dev"))),
        check_vma=False,
    )
```

profile of v0, /device:TPU:1, one launch (start us, length us, event | category | flops | bytes accessed | tf_op | source)
XLA Modules:
  0.0 836.6 jit_solution(16834892905847499718)
XLA Ops:
  7.2 1.0 copy.40
  8.2 0.7 copy-done.7
  8.8 0.6 fusion.47
  12.0 0.6 copy-done.8
  12.7 0.7 fusion.46
  15.9 2.6 dynamic-slice_select_fusion
  18.7 256.7 %all-reduce.6.cloned.1.call-done = f32[440,256]{1,0:T(8,128)} async-done(((f32[440,256]{1,0:T(8,128)}), f32[440,256]{1,0:T(8,128)}) %all-reduce.6.cloned.1.call-update) | async-done | bytes 450576 | tf_op jit(solution)/shard_map/psum | solution.py:15
  275.4 1.2 multiply_reduce_fusion.2
  276.6 1.0 fusion.12
  277.8 11.7 %cholesky.130 = f32[128,128]{1,0:T(8,128)S(1)} custom-call(f32[128,128]{1,0:T(8,128)S(1)} %cholesky.194), custom_call_target="Cholesky" | custom-call | tf_op jit(solution)/shard_map/jit(cholesky)/cholesky | solution.py:36
  289.6 9.8 %custom-call.17 = f32[1,128,128]{1,2,0:T(8,128)S(1)} custom-call(f32[1,128,128]{2,1,0:T(8,128)S(1)} %get-tuple-element.68), custom_call_target="InvertDiagBlocksLowerTriangular" | custom-call | tf_op jit(solution)/shard_map/jit(cholesky)/cholesky | solution.py:36
  299.9 11.7 %cholesky.147 = f32[128,128]{1,0:T(8,128)S(1)} custom-call(f32[128,128]{1,0:T(8,128)S(1)} %convolution_subtract_fusion.7), custom_call_target="Cholesky" | custom-call | tf_op jit(solution)/shard_map/jit(cholesky)/cholesky | solution.py:36
  311.6 1.5 fusion.7
  313.2 1.3 convolution_bitcast_fusion
  314.6 0.7 compare_reduce_fusion.2
  316.7 4.0 while.8
  316.7 0.6 fusion.79
  317.4 1.4 bitcast_dynamic-update-slice_fusion.4
  318.7 0.6 fusion.79
  319.4 1.4 bitcast_dynamic-update-slice_fusion.4
  320.7 19.7 %custom-call.19 = f32[2,128,128]{1,2,0:T(8,128)S(1)} custom-call(f32[2,128,128]{2,1,0:T(8,128)S(1)} %get-tuple-element.34), custom_call_target="InvertDiagBlocksLowerTriangular" | custom-call | tf_op jit(solution)/shard_map/triangular_solve/custom-call.4 | solution.py:38
  340.4 226.3 %all-reduce.10.cloned.1.call-done = (f32[147,256]{1,0:T(8,128)}, f32[440,256]{1,0:T(8,128)}) async-done(((f32[147,256]{1,0:T(8,128)}, f32[440,256]{1,0:T(8,128)}), (f32[147,256]{1,0:T(8,128)}, f32[440,256]{1,0:T(8,128)})) %all-reduce.10.cloned.1.call-update) | async-done | bytes 601104 | tf_op jit(solution)/shard_map/psum | solution.py:63
  566.7 1.2 multiply_reduce_fusion.1
  567.9 1.2 fusion.5
  569.1 1.0 fusion.17
  570.1 0.6 multiply_reduce_fusion.4
  571.1 0.3 convolution_subtract_fusion.5
  571.6 0.3 fusion.34
  573.2 0.5 convolution_subtract_fusion.1
  573.7 1.3 fusion.48
  575.3 11.7 %cholesky.164 = f32[128,128]{1,0:T(8,128)S(1)} custom-call(f32[128,128]{1,0:T(8,128)S(1)} %cholesky.197), custom_call_target="Cholesky" | custom-call | tf_op jit(solution)/shard_map/jit(cholesky)/cholesky | solution.py:36
  587.1 9.8 %custom-call.20 = f32[1,128,128]{1,2,0:T(8,128)S(1)} custom-call(f32[1,128,128]{2,1,0:T(8,128)S(1)} %get-tuple-element.64), custom_call_target="InvertDiagBlocksLowerTriangular" | custom-call | tf_op jit(solution)/shard_map/jit(cholesky)/cholesky | solution.py:36
  597.3 11.9 %cholesky.181 = f32[128,128]{1,0:T(8,128)S(1)} custom-call(f32[128,128]{1,0:T(8,128)S(1)} %convolution_subtract_fusion.6), custom_call_target="Cholesky" | custom-call | tf_op jit(solution)/shard_map/jit(cholesky)/cholesky | solution.py:36
  609.3 0.7 compare_reduce_fusion
  611.3 4.0 while.9
  611.3 0.6 fusion.80
  611.9 1.4 bitcast_dynamic-update-slice_fusion.5
  613.3 0.6 fusion.80
  613.9 1.4 bitcast_dynamic-update-slice_fusion.5
  615.3 19.7 %custom-call.22 = f32[2,128,128]{1,2,0:T(8,128)S(1)} custom-call(f32[2,128,128]{2,1,0:T(8,128)S(1)} %get-tuple-element.36), custom_call_target="InvertDiagBlocksLowerTriangular" | custom-call | tf_op jit(solution)/shard_map/triangular_solve/custom-call.4 | solution.py:38
  635.1 1.5 dynamic_update_slice.6
  636.6 185.7 %all-reduce.8.cloned.1.call-done = f32[147,256]{1,0:T(8,128)} async-done(((f32[147,256]{1,0:T(8,128)}), f32[147,256]{1,0:T(8,128)}) %all-reduce.8.cloned.1.call-update) | async-done | bytes 150544 | tf_op jit(solution)/shard_map/psum | solution.py:63
  822.3 1.2 fusion.20
  824.7 0.3 fusion.35
  825.0 0.6 multiply_reduce_fusion.3
  826.4 1.2 convolution_subtract_fusion
  827.7 1.5 dynamic_update_slice.7
  829.2 0.7 copy-done.4
  (58 shorter events, 4.5 us)
Async XLA Ops:
  7.2 268.3 %all-reduce.6.cloned.1.call-start = ((), (), s32[]{:S(2)}) async-start(), calls=%async_computation | async-start | bytes 901120 | tf_op jit(solution)/shard_map/psum | solution.py:15
  8.2 0.7 copy-start.7
  12.0 0.7 copy-start.8
  15.9 2.7 copy-start
  18.5 548.2 %all-reduce.10.cloned.1.call-start = ((), (), s32[]{:S(2)}) async-start(), calls=%async_computation.2 | async-start | bytes 1212416 | tf_op jit(solution)/shard_map/psum | solution.py:63
  275.4 1.2 copy-start.2
  311.6 1.6 copy-start.3
  314.5 507.8 %all-reduce.8.cloned.1.call-start = ((), (), s32[]{:S(2)}) async-start(), calls=%async_computation.1 | async-start | bytes 311296 | tf_op jit(solution)/shard_map/psum | solution.py:63
  566.7 1.2 copy-start.1
  569.1 1.0 copy-start.6
  822.3 1.2 copy-start.5
  829.2 0.7 copy-start.4
Sparse Core Ops, SparseCore 0:
  18.7 256.7 all-reduce.5
  314.7 252.0 all-reduce.9
  575.2 247.0 all-reduce.7
where the time goes:
time: 851 us; the launch traced here: 837 us
  waiting for transfers between devices  669 us (79%)
  other arithmetic  114 us (13%)
  between operations  23.4 us (3%)
  local copies, waits for them, and re-layouts  15.5 us (2%)
  matrix products  14.5 us (2%)
    psum x2, waiting for transfers between devices, body(): grad = lax.psum(contract(residual, tile), ('group', 'dev'))  412 us
    psum x1, waiting for transfers between devices, spread_2(): return lax.psum(jnp.where(mine, value, jnp.zeros_like(value)), axis)  257 us
    another operation x12, other arithmetic, precondition(): lower = jnp.linalg.cholesky(gram)  68.2 us
    another operation x5, other arithmetic, precondition(): lax.linalg.triangular_solve(lower, inner, left_side=True, lower=True, tra...  39.4 us
  transfers between devices with their start and end apart: 3, of which 3 were waited for; matrix products, arithmetic and copies ran while one was open for 10% of the time, Pallas kernels for 0%

commit v1 on v0

v1 whole, which is shorter than its diff:
```python
import functools
import itertools

import jax
import jax.numpy as jnp
from jax import lax
from jax.experimental import pallas as pl
from jax.experimental.pallas import tpu as pltpu
from jax.sharding import PartitionSpec as P

BLOCK = 256
LANES = 128
AXES = ("group", "dev")

VMEM_LIMIT = 24 << 20
SWEEP_FLOPS = 4_000_000_000

ridge = 2.0
step_norm = 1.5

VMEM = pl.BlockSpec(memory_space=pltpu.VMEM)
SMEM = pl.BlockSpec(memory_space=pltpu.SMEM)


def rings():
    ys, cores, zs, xs = range(4), range(2), range(8), range(4)
    at = lambda y, c, z, x: (y * 2 + c) * 32 + z * 4 + x
    planes = [[at(y, c, z, x) for y, x in itertools.product(ys, xs)] for c, z in itertools.product(cores, zs)]
    lines = [[at(y, c, z, x) for z in zs] for y, c, x in itertools.product(ys, cores, xs)]
    partners = [(at(y, c, z, x), at(y, 1 - c, z, x)) for y, c, z, x in itertools.product(ys, cores, zs, xs)]
    return planes, lines, partners


PLANES, LINES, PARTNERS = rings()


def swap(value):
    return lax.ppermute(value, AXES, PARTNERS)


def exchange(value, groups):
    return lax.all_to_all(value, AXES, 0, 0, tiled=True, axis_index_groups=groups)


def scatter_sum(value, groups):
    n = len(groups[0])
    parts = exchange(value, groups)
    return jnp.sum(parts.reshape(n, value.shape[0] // n, value.shape[1]), axis=0)


def replicate(value, n):
    return jnp.broadcast_to(value[None], (n,) + value.shape).reshape(n * value.shape[0], value.shape[1])


def all_sum(value, groups):
    return scatter_sum(replicate(value, len(groups[0])), groups)


def collect(value, groups):
    return exchange(replicate(value, len(groups[0])), groups)


def all_reduce(kept, sent):
    value = kept + swap(sent)
    value = scatter_sum(value, PLANES)
    value = all_sum(value, LINES)
    return collect(value, PLANES)


def dot(left, right, dims):
    return lax.dot_general(left, right, (dims, ((), ())), precision=lax.Precision.HIGHEST, preferred_element_type=jnp.float32)


def up(count, to):
    return -(-count // to) * to


def params():
    return pltpu.CompilerParams(vmem_limit_bytes=VMEM_LIMIT)


def core():
    return lax.rem(lax.axis_index("group"), 2)


def in_order(mine, other):
    first = core() == 0
    return jnp.where(first, mine, other), jnp.where(first, other, mine)


def stage_kernel(owners, offsets, points, kept, sent):
    here = lax.axis_index(AXES)
    features, width = points.shape
    for step, out in ((core(), kept), (1 - core(), sent)):

        @pl.when(owners[step] == here)
        def _():
            turned = pltpu.roll(points[...], lax.rem(width - offsets[step], width), axis=1)
            out[:features, :] = turned[:, :LANES]
            out[features : 2 * features, :] = turned[:, LANES : 2 * LANES]
            out[2 * features :, :] = jnp.zeros((out.shape[0] - 2 * features, LANES), jnp.float32)

        @pl.when(owners[step] != here)
        def _():
            out[...] = jnp.zeros(out.shape, jnp.float32)


def stage(owners, offsets, points):
    half = jax.ShapeDtypeStruct((up(2 * points.shape[0], 128), LANES), jnp.float32)
    return pl.pallas_call(
        stage_kernel,
        out_shape=(half, half),
        in_specs=[SMEM, SMEM, VMEM],
        out_specs=(VMEM, VMEM),
        name="stage",
        compiler_params=params(),
    )(owners, offsets, points)


def kernel_values(left, right):
    features = left.shape[0]
    down = jnp.broadcast_to(jnp.sum(left * left, axis=0, keepdims=True), (8, left.shape[1])).T[:, :1]
    along = jnp.sum(right * right, axis=0, keepdims=True)
    return jnp.exp((2.0 * dot(left, right, ((0,), (0,))) - down - along) * (1.0 / features))


def tiles_kernel(mine, other, points, residual, tiles, kept, sent):
    features, classes = points.shape[0], residual.shape[0]
    rows = up(classes, 8)
    pieces = [half[i * features : (i + 1) * features, :] for half in in_order(mine[...], other[...]) for i in range(2)]
    tiles[...] = kernel_values(jnp.concatenate(pieces, axis=1), points[...])
    grads = dot(residual[...], tiles[...], ((1,), (1,)))
    overlap = dot(tiles[:BLOCK, :], tiles[BLOCK:, :], ((1,), (1,)))
    gap = jnp.zeros((rows - classes, LANES), jnp.float32)
    halves = []
    for step in range(2):
        left, right = (grads[:, (2 * step + i) * LANES : (2 * step + i + 1) * LANES] for i in range(2))
        end = jnp.zeros((kept.shape[0] - 2 * rows - BLOCK, LANES), jnp.float32)
        halves.append((left, right, overlap[:, step * LANES : (step + 1) * LANES], end))
    for out, own in ((kept, 0), (sent, 1)):
        left, right, products, end = (in_order(a, b)[own] for a, b in zip(*halves))
        out[:classes, :] = left
        out[classes:rows, :] = gap
        out[rows : rows + classes, :] = right
        out[rows + classes : 2 * rows, :] = gap
        out[2 * rows : 2 * rows + BLOCK, :] = products
        out[2 * rows + BLOCK :, :] = end


def make_tiles(mine, other, points, residual):
    width, rows = points.shape[1], up(residual.shape[0], 8)
    half = jax.ShapeDtypeStruct((up(2 * rows + BLOCK, 128), LANES), jnp.float32)
    return pl.pallas_call(
        tiles_kernel,
        out_shape=(jax.ShapeDtypeStruct((2 * BLOCK, width), jnp.float32), half, half),
        in_specs=[VMEM] * 4,
        out_specs=(VMEM,) * 3,
        name="tiles",
        compiler_params=params(),
    )(mine, other, points, residual)


def gram_kernel(features, mine, gram):
    block = jnp.concatenate([mine[i * features : (i + 1) * features, :] for i in range(2)], axis=1)
    diagonal = lax.broadcasted_iota(jnp.int32, gram.shape, 0) == lax.broadcasted_iota(jnp.int32, gram.shape, 1)
    gram[...] = kernel_values(block, block) + jnp.where(diagonal, ridge, 0.0)


def make_gram(mine, features):
    return pl.pallas_call(
        functools.partial(gram_kernel, features),
        out_shape=jax.ShapeDtypeStruct((BLOCK, BLOCK), jnp.float32),
        in_specs=[VMEM],
        out_specs=VMEM,
        name="gram",
        compiler_params=params(),
        cost_estimate=pl.CostEstimate(flops=SWEEP_FLOPS // 4, bytes_accessed=1 << 20, transcendentals=0),
    )(mine)


def inverse_2(a, b, d):
    r = 1.0 / (a * d - b * b)
    return d * r, -b * r, a * r


def inverse_4(v):
    pair = range(2)
    x, y, z = inverse_2(v[0][0], v[0][1], v[1][1])
    corner = [[x, y], [y, z]]
    right = [[v[i][2 + j] for j in pair] for i in pair]
    u = [[corner[i][0] * right[0][j] + corner[i][1] * right[1][j] for j in pair] for i in pair]
    rest = [[v[2 + i][2 + j] - (right[0][i] * u[0][j] + right[1][i] * u[1][j]) for j in pair] for i in pair]
    e, f, g = inverse_2(rest[0][0], rest[0][1], rest[1][1])
    last = [[e, f], [f, g]]
    w = [[u[i][0] * last[0][j] + u[i][1] * last[1][j] for j in pair] for i in pair]
    first = [[corner[i][j] + w[i][0] * u[j][0] + w[i][1] * u[j][1] for j in pair] for i in pair]
    return [
        [first[0][0], first[0][1], -w[0][0], -w[0][1]],
        [first[0][1], first[1][1], -w[1][0], -w[1][1]],
        [-w[0][0], -w[1][0], e, f],
        [-w[0][1], -w[1][1], f, g],
    ]


def negative_inverse(p):
    n = p.shape[0]
    down = lax.broadcasted_iota(jnp.int32, (n, n), 0)
    along = lax.broadcasted_iota(jnp.int32, (n, n), 1)
    four = range(4)
    for j in range(0, n, 4):
        cols = [jnp.broadcast_to(p[:, j + i : j + i + 1], (n, n)) for i in four]
        rows = [p[j + i : j + i + 1, :] for i in four]
        w = inverse_4([[cols[k][j + i : j + i + 1, :] for k in four] for i in four])
        past = (along[:1] >= j) & (along[:1] < j + 4)
        rows = [jnp.where(past, 0.0, row) for row in rows]
        scaled = [sum(w[i][k] * rows[k] for k in four) for i in four]
        for i in four:
            p = p - cols[i] * scaled[i]
        for k in four:
            fresh = sum(cols[i] * w[i][k] for i in four)
            p = jnp.where(along == j + k, fresh, p)
        for i in four:
            row = scaled[i]
            for k in four:
                row = jnp.where(along[:1] == j + k, -w[i][k], row)
            p = jnp.where(down == j + i, row, p)
    return p


def sweep_kernel(first, last, size, source, out):
    n = out.shape[1]
    for at in range(first, last, size):
        along = lax.broadcasted_iota(jnp.int32, (size, n), 1)
        past = (along >= at) & (along < at + size)
        rows = source[at : at + size, :]
        pivot = negative_inverse(rows[:, at : at + size])
        panel = jnp.where(past, 0.0, rows)
        scaled = dot(pivot, panel, ((1,), (0,)))
        wide = jnp.pad(pivot, ((0, 0), (at, n - at - size)))
        fresh = jnp.where(past, wide, -scaled)
        out[...] = source[...] + dot(panel, scaled, ((0,), (0,)))
        out[at : at + size, :] = fresh
        out[:, at : at + size] = fresh.T
        source = out


def sweep(gram, first, last, size=64):
    return pl.pallas_call(
        functools.partial(sweep_kernel, first, last, size),
        out_shape=jax.ShapeDtypeStruct(gram.shape, gram.dtype),
        in_specs=[VMEM],
        out_specs=VMEM,
        name="sweep",
        compiler_params=params(),
        cost_estimate=pl.CostEstimate(flops=SWEEP_FLOPS * (last - first) // 64, bytes_accessed=1 << 20, transcendentals=0),
    )(gram)


def finish_kernel(
    owners, offsets, my_sums, other_sums, my_inverse, other_inverse, tiles, residual, coeffs, new_residual, new_coeffs
):
    here = lax.axis_index(AXES)
    classes, width = residual.shape
    rows = up(classes, 8)
    sums = in_order(my_sums[...], other_sums[...])
    inverses = in_order(my_inverse[...], other_inverse[...])
    grads = [jnp.concatenate([half[:rows, :], half[rows : 2 * rows, :]], axis=1) for half in sums]
    overlap = jnp.concatenate([half[2 * rows : 2 * rows + BLOCK, :] for half in sums], axis=1)

    def direction(grad, inverse):
        scale = step_norm / jnp.sqrt(jnp.sum(grad * grad) * (1.0 / (classes * BLOCK)) + 1e-06)
        return dot(grad, inverse, ((1,), (0,))) * -scale

    delta0 = direction(grads[0], inverses[0])
    delta1 = direction(grads[1] - dot(delta0, overlap, ((1,), (0,))), inverses[1])
    deltas = [delta[:classes] for delta in (delta0, delta1)]
    new_residual[...] = residual[...] - dot(jnp.concatenate(deltas, axis=1), tiles[...], ((1,), (0,)))
    new_coeffs[...] = coeffs[...]
    for step in range(2):

        @pl.when(owners[step] == here)
        def _():
            wide = jnp.concatenate([deltas[step], jnp.zeros((classes, width - BLOCK), jnp.float32)], axis=1)
            new_coeffs[...] = new_coeffs[...] + pltpu.roll(wide, offsets[step], axis=1)


def finish(owners, offsets, *arrays):
    residual, coeffs = arrays[-2:]
    return pl.pallas_call(
        finish_kernel,
        out_shape=(jax.ShapeDtypeStruct(residual.shape, jnp.float32), jax.ShapeDtypeStruct(coeffs.shape, jnp.float32)),
        in_specs=[SMEM, SMEM] + [VMEM] * 7,
        out_specs=(VMEM, VMEM),
        name="finish",
        compiler_params=params(),
    )(owners, offsets, *arrays)


def body(points, residual, coeffs, owners, offsets):
    mine = all_reduce(*stage(owners, offsets, points))
    tiles, kept, sent = make_tiles(mine, swap(mine), points, residual)
    inverse = make_gram(mine, points.shape[0])
    for at in range(0, BLOCK, 64):
        inverse = sweep(inverse, at, at + 64)
    sums = all_reduce(kept, sent)
    return finish(owners, offsets, sums, swap(sums), inverse, swap(inverse), tiles, residual, coeffs)


def solution(mesh):
    split = P(None, AXES)
    return jax.shard_map(
        body,
        mesh=mesh,
        in_specs=(split, split, split, P(), P()),
        out_specs=(split, split),
        check_vma=False,
    )
```

time: 851 us -> 114 us (0.13); the launches traced: 837 us -> 113 us
  waiting for transfers between devices: 669 us -> 19.6 us
  other arithmetic: 114 us -> 0.89 us
  blocking collectives: 0 us -> 44.1 us
  between operations: 23.4 us -> 0.8 us
  starting transfers between devices: 0.12 us -> 22.6 us
  Pallas kernels: 0 us -> 21.5 us
  matrix products: 14.5 us -> 0 us
  local copies, waits for them, and re-layouts: 15.5 us -> 3.97 us
    psum x3 -> x0, waiting for transfers between devices: 669 us -> none  [the longest x2 412 us: body(): grad = lax.psum(contract(residual, tile), ('group', 'dev'))]
    another operation x17 -> x0, other arithmetic: 108 us -> none  [the longest x12 68.2 us: precondition(): lower = jnp.linalg.cholesky(gram)]
    all_to_all x0 -> x3, blocking collectives: none -> 44.1 us  [exchange(): lax.all_to_all(value, AXES, 0, 0, tiled=True, axis_index_groups=groups)]
    pallas_call x0 -> x8, Pallas kernels: none -> 21.5 us  [the longest x4 13.4 us: sweep(): pl.pallas_call(functools.partial(sweep_kernel, first, last, size), out_sh...]
    all_to_all x0 -> x3, waiting for transfers between devices: none -> 14.7 us  [exchange(): lax.all_to_all(value, AXES, 0, 0, tiled=True, axis_index_groups=groups)]
    ppermute x0 -> x5, starting transfers between devices: none -> 12 us  [swap(): return lax.ppermute(value, AXES, PARTNERS)]
    all_to_all x0 -> x3, starting transfers between devices: none -> 10.6 us  [exchange(): lax.all_to_all(value, AXES, 0, 0, tiled=True, axis_index_groups=groups)]
    dot_general x8 -> x0, matrix products: 9.1 us -> none  [the longest x4 4.74 us: kernel_tile(): lax.dot_general(block, cols, (((0,), (0,)), ((), ())), precision=lax.Prec...]
  transfers between devices with their start and end apart: 3 -> 8, of which waited for: 3 -> 7; matrix products, arithmetic and copies ran while one was open for 10% -> 0% of each run, Pallas kernels for 0% -> 12%
where the time goes in v1:
time: 114 us; the launch traced here: 113 us
  blocking collectives  44.1 us (39%)
  starting transfers between devices  22.6 us (20%)
  Pallas kernels  21.5 us (19%)
  waiting for transfers between devices  19.6 us (17%)
  local copies, waits for them, and re-layouts  3.97 us (3%)
    all_to_all x3, blocking collectives, exchange(): lax.all_to_all(value, AXES, 0, 0, tiled=True, axis_index_groups=groups)  44.1 us
    all_to_all x3, waiting for transfers between devices, exchange(): lax.all_to_all(value, AXES, 0, 0, tiled=True, axis_index_groups=groups)  14.7 us
    pallas_call x4, Pallas kernels, sweep(): pl.pallas_call(functools.partial(sweep_kernel, first, last, size), out_sh...  13.4 us
    ppermute x5, starting transfers between devices, swap(): return lax.ppermute(value, AXES, PARTNERS)  12 us
    all_to_all x3, starting transfers between devices, exchange(): lax.all_to_all(value, AXES, 0, 0, tiled=True, axis_index_groups=groups)  10.6 us
    ppermute x5, waiting for transfers between devices, swap(): return lax.ppermute(value, AXES, PARTNERS)  4.92 us
    pallas_call x1, Pallas kernels, make_tiles(): pl.pallas_call(tiles_kernel, out_shape=(jax.ShapeDtypeStruct((2 * BLOCK,...  3.72 us
    pallas_call x1, Pallas kernels, finish(): pl.pallas_call(finish_kernel, out_shape=(jax.ShapeDtypeStruct(residual.sh...  2.94 us
  transfers between devices with their start and end apart: 8, of which 7 were waited for; matrix products, arithmetic and copies ran while one was open for 0% of the time, Pallas kernels for 12%

profile of v1, /device:TPU:1, one launch (start us, length us, event | category | flops | bytes accessed | tf_op | source)
XLA Modules:
  0.0 113.5 jit_solution(10031213422361566491)
XLA Ops:
  0.6 0.0 copy-start
  0.6 1.2 %copy-done = f32[440,512]{1,0:T(8,128)S(1)} copy-done((f32[440,512]{1,0:T(8,128)S(1)}, f32[440,512]{1,0:T(8,128)}, u32[]{:S(2)}) %copy-start) | copy-done | bytes 901144
  1.8 0.0 copy-start.4
  1.8 0.7 copy-done.4
  2.5 0.0 copy-start.6
  2.5 0.7 copy-done.6
  3.1 0.6 stage.1
  3.8 3.3 %collective-permute-start = (f32[896,128]{1,0:T(8,128)S(1)}, f32[896,128]{1,0:T(8,128)S(1)}, u32[]{:S(2)}, u32[]{:S(2)}) collective-permute-start(f32[896,128]{1,0:T(8,128)S(1)} %get-tuple-element.8), channel_id=1, source_target_pairs={{0,32},{1,33},{2,34},{3,35},{4,36},{5,37},{6,38},{7,39},{8,40},{9,... | collective-permute-start | bytes 1376264 | tf_op jit(solution)/shard_map/ppermute | solution.py:38
  7.1 1.4 %collective-permute-done = f32[896,128]{1,0:T(8,128)S(1)} collective-permute-done((f32[896,128]{1,0:T(8,128)S(1)}, f32[896,128]{1,0:T(8,128)S(1)}, u32[]{:S(2)}, u32[]{:S(2)}) %collective-permute-start) | collective-permute-done | bytes 458784 | tf_op jit(solution)/shard_map/ppermute | solution.py:38
  8.5 14.8 %all_to_all.46 = f32[16,56,128]{2,1,0:T(8,128)S(1)} all-to-all(f32[16,56,128]{2,1,0:T(8,128)S(1)} %bitcast.9), channel_id=1, replica_groups={{0,1,2,3,64,65,66,67,128,129,130,131,192,193,194,195},{4,5,6,7,68,69,70..., dimensions={0} | all-to-all | bytes 917504 | tf_op jit(solution)/shard_map/all_to_all | solution.py:42
  23.4 17.1 %all_to_all.47 = f32[8,56,128]{2,1,0:T(8,128)S(1)} all-to-all(f32[8,56,128]{2,1,0:T(8,128)S(1)} %broadcast_in_dim.8), channel_id=1, replica_groups={{0,4,8,12,16,20,24,28},{1,5,9,13,17,21,25,29},{2,6,10,14,18,22,26,30},{..., dimensions={0} | all-to-all | bytes 458752 | tf_op jit(solution)/shard_map/all_to_all | solution.py:42
  40.5 0.0 copy-start.1
  40.5 0.0 copy-start.2
  40.5 12.2 %all_to_all.48 = f32[16,56,128]{2,1,0:T(8,128)S(1)} all-to-all(f32[16,56,128]{2,1,0:T(8,128)S(1)} %broadcast_in_dim.9), channel_id=1, replica_groups={{0,1,2,3,64,65,66,67,128,129,130,131,192,193,194,195},{4,5,6,7,68,69,70..., dimensions={0} | all-to-all | bytes 917504 | tf_op jit(solution)/shard_map/all_to_all | solution.py:42
  52.8 4.2 %collective-permute-start.1 = (f32[896,128]{1,0:T(8,128)S(1)}, f32[896,128]{1,0:T(8,128)S(1)}, u32[]{:S(2)}, u32[]{:S(2)}) collective-permute-start(f32[896,128]{1,0:T(8,128)S(1)} %bitcast.4), channel_id=1, source_target_pairs={{0,32},{1,33},{2,34},{3,35},{4,36},{5,37},{6,38},{7,39},{8,40},{9,... | collective-permute-start | bytes 1376264 | tf_op jit(solution)/shard_map/ppermute | solution.py:38
  57.0 1.4 %collective-permute-done.1.other = f32[896,128]{1,0:T(8,128)S(1)} collective-permute-done((f32[896,128]{1,0:T(8,128)S(1)}, f32[896,128]{1,0:T(8,128)S(1)}, u32[]{:S(2)}, u32[]{:S(2)}) %collective-permute-start.1) | collective-permute-done | bytes 458784 | tf_op jit(solution)/shard_map/ppermute | solution.py:38
  58.4 0.0 copy-done.1
  58.5 0.0 copy-done.2
  58.5 3.7 %tiles.1 = (f32[512,512]{1,0:T(8,128)S(1)}, f32[640,128]{1,0:T(8,128)S(1)}, f32[640,128]{1,0:T(8,128)S(1)}) custom-call(f32[896,128]{1,0:T(8,128)S(1)} %bitcast.5, f32[896,128]{1,0:T(8,128)S(1)} %collective-permute-done.1.other, f32[440,512]{1,0:T(8,128)S(1)} %copy-done.1, f32[147,512]{1,0:T(8,128)S(1)} %copy-done.2), custom_call_target="tpu_custom_call" | custom-call | tf_op jit(solution)/shard_map/tiles/pallas_call | solution.py:153
  62.2 0.5 collective-permute-start.2
  62.6 0.7 gram.1.source
  63.4 0.5 collective-permute-done.2
  63.9 0.8 add.7
  64.7 3.5 %all-to-all-start.3 = ((f32[16,40,128]{2,1,0:T(8,128)}), f32[16,40,128]{2,1,0:T(8,128)S(1)}, u32[]{:S(2)}, u32[]{:S(2)}) async-start(f32[16,40,128]{2,1,0:T(8,128)} %bitcast.2), calls=%async_computation.3 | async-start | bytes 655360 | tf_op jit(solution)/shard_map/all_to_all | solution.py:42
  68.2 3.3 %sweep.4.source = f32[256,256]{1,0:T(8,128)S(1)} custom-call(f32[256,256]{1,0:T(8,128)S(1)} %gram.1.source), custom_call_target="tpu_custom_call" | custom-call | flops 4000000000 | bytes 1048576 | tf_op jit(solution)/shard_map/sweep/pallas_call | solution.py:248
  71.5 5.7 %all-to-all-done.3 = f32[16,40,128]{2,1,0:T(8,128)S(1)} async-done(((f32[16,40,128]{2,1,0:T(8,128)}), f32[16,40,128]{2,1,0:T(8,128)S(1)}, u32[]{:S(2)}, u32[]{:S(2)}) %all-to-all-start.3) | async-done | bytes 327712 | tf_op jit(solution)/shard_map/all_to_all | solution.py:42
  77.2 0.7 broadcast_in_dim.10
  77.9 3.6 %all-to-all-start.4 = ((f32[8,40,128]{2,1,0:T(8,128)}), f32[8,40,128]{2,1,0:T(8,128)S(1)}, u32[]{:S(2)}, u32[]{:S(2)}) async-start(f32[8,40,128]{2,1,0:T(8,128)} %broadcast_in_dim.10), calls=%async_computation.4 | async-start | bytes 327680 | tf_op jit(solution)/shard_map/all_to_all | solution.py:42
  81.5 3.4 %sweep.5.source = f32[256,256]{1,0:T(8,128)S(1)} custom-call(f32[256,256]{1,0:T(8,128)S(1)} %sweep.4.source), custom_call_target="tpu_custom_call" | custom-call | flops 4000000000 | bytes 1048576 | tf_op jit(solution)/shard_map/sweep/pallas_call | solution.py:248
  84.9 4.5 %all-to-all-done.4 = f32[8,40,128]{2,1,0:T(8,128)S(1)} async-done(((f32[8,40,128]{2,1,0:T(8,128)}), f32[8,40,128]{2,1,0:T(8,128)S(1)}, u32[]{:S(2)}, u32[]{:S(2)}) %all-to-all-start.4) | async-done | bytes 163872 | tf_op jit(solution)/shard_map/all_to_all | solution.py:42
  89.4 0.7 broadcast_in_dim.11
  90.1 3.5 %all-to-all-start.5 = ((f32[16,40,128]{2,1,0:T(8,128)}), f32[16,40,128]{2,1,0:T(8,128)S(1)}, u32[]{:S(2)}, u32[]{:S(2)}) async-start(f32[16,40,128]{2,1,0:T(8,128)} %broadcast_in_dim.11), calls=%async_computation.5 | async-start | bytes 655360 | tf_op jit(solution)/shard_map/all_to_all | solution.py:42
  93.7 3.3 %sweep.6.source = f32[256,256]{1,0:T(8,128)S(1)} custom-call(f32[256,256]{1,0:T(8,128)S(1)} %sweep.5.source), custom_call_target="tpu_custom_call" | custom-call | flops 4000000000 | bytes 1048576 | tf_op jit(solution)/shard_map/sweep/pallas_call | solution.py:248
  97.0 4.6 %all-to-all-done.5 = f32[16,40,128]{2,1,0:T(8,128)S(1)} async-done(((f32[16,40,128]{2,1,0:T(8,128)}), f32[16,40,128]{2,1,0:T(8,128)S(1)}, u32[]{:S(2)}, u32[]{:S(2)}) %all-to-all-start.5) | async-done | bytes 327712 | tf_op jit(solution)/shard_map/all_to_all | solution.py:42
  101.5 0.0 copy-start.3
  101.5 3.9 %collective-permute-start.3 = (f32[640,128]{1,0:T(8,128)S(1)}, f32[640,128]{1,0:T(8,128)S(1)}, u32[]{:S(2)}, u32[]{:S(2)}) collective-permute-start(f32[640,128]{1,0:T(8,128)S(1)} %bitcast.7), channel_id=1, source_target_pairs={{0,32},{1,33},{2,34},{3,35},{4,36},{5,37},{6,38},{7,39},{8,40},{9,... | collective-permute-start | bytes 983048 | tf_op jit(solution)/shard_map/ppermute | solution.py:38
  105.4 3.4 %sweep.7.my_inverse = f32[256,256]{1,0:T(8,128)S(1)} custom-call(f32[256,256]{1,0:T(8,128)S(1)} %sweep.6.source), custom_call_target="tpu_custom_call" | custom-call | flops 4000000000 | bytes 1048576 | tf_op jit(solution)/shard_map/sweep/pallas_call | solution.py:248
  108.8 0.0 copy-start.5
  108.9 0.0 copy-start.7
  108.9 0.1 collective-permute-start.4
  109.0 1.5 %collective-permute-done.4.other_inverse = f32[256,256]{1,0:T(8,128)S(1)} collective-permute-done((f32[256,256]{1,0:T(8,128)S(1)}, f32[256,256]{1,0:T(8,128)S(1)}, u32[]{:S(2)}, u32[]{:S(2)}) %collective-permute-start.4) | collective-permute-done | bytes 262176 | tf_op jit(solution)/shard_map/ppermute | solution.py:38
  110.5 0.0 collective-permute-done.3.other_sums
  110.5 0.0 copy-done.3
  110.5 0.0 copy-done.5
  110.5 0.0 copy-done.7
  110.5 2.9 %finish.1 = (f32[147,512]{1,0:T(8,128)}, f32[147,512]{1,0:T(8,128)}) custom-call(s32[2]{0:T(128)S(1)} %copy-done.5, s32[2]{0:T(128)S(1)} %copy-done.7, f32[640,128]{1,0:T(8,128)S(1)} %bitcast.8, f32[640,128]{1,0:T(8,128)S(1)} %collective-permute-done.3.other_sums, f32[256,256]{1,0:T(8,128)S(1)} %sweep.7.my_inverse, ...), custom_call_target="tpu_custom_call" | custom-call | tf_op jit(solution)/shard_map/finish/pallas_call | solution.py:289
  (7 shorter events, 0.2 us)
Async XLA Ops:
  0.6 1.2 %copy-start = (f32[440,512]{1,0:T(8,128)S(1)}, f32[440,512]{1,0:T(8,128)}, u32[]{:S(2)}) copy-start(f32[440,512]{1,0:T(8,128)} %points.3) | copy-start | bytes 2703364
  1.8 0.7 copy-start.4
  2.5 0.7 copy-start.6
  3.8 4.7 %collective-permute-start = (f32[896,128]{1,0:T(8,128)S(1)}, f32[896,128]{1,0:T(8,128)S(1)}, u32[]{:S(2)}, u32[]{:S(2)}) collective-permute-start(f32[896,128]{1,0:T(8,128)S(1)} %get-tuple-element.8), channel_id=1, source_target_pairs={{0,32},{1,33},{2,34},{3,35},{4,36},{5,37},{6,38},{7,39},{8,40},{9,... | collective-permute-start | bytes 1376264 | tf_op jit(solution)/shard_map/ppermute | solution.py:38
  40.5 18.0 %copy-start.1 = (f32[440,512]{1,0:T(8,128)S(1)}, f32[440,512]{1,0:T(8,128)}, u32[]{:S(2)}) copy-start(f32[440,512]{1,0:T(8,128)} %points.3) | copy-start | bytes 2703364
  40.5 17.9 %copy-start.2 = (f32[147,512]{1,0:T(8,128)S(1)}, f32[147,512]{1,0:T(8,128)}, u32[]{:S(2)}) copy-start(f32[147,512]{1,0:T(8,128)} %residual.3) | copy-start | bytes 903172
  52.8 5.7 %collective-permute-start.1 = (f32[896,128]{1,0:T(8,128)S(1)}, f32[896,128]{1,0:T(8,128)S(1)}, u32[]{:S(2)}, u32[]{:S(2)}) collective-permute-start(f32[896,128]{1,0:T(8,128)S(1)} %bitcast.4), channel_id=1, source_target_pairs={{0,32},{1,33},{2,34},{3,35},{4,36},{5,37},{6,38},{7,39},{8,40},{9,... | collective-permute-start | bytes 1376264 | tf_op jit(solution)/shard_map/ppermute | solution.py:38
  62.2 1.7 %collective-permute-start.2 = (f32[640,128]{1,0:T(8,128)S(1)}, f32[640,128]{1,0:T(8,128)S(1)}, u32[]{:S(2)}, u32[]{:S(2)}) collective-permute-start(f32[640,128]{1,0:T(8,128)S(1)} %get-tuple-element.10), channel_id=1, source_target_pairs={{0,32},{1,33},{2,34},{3,35},{4,36},{5,37},{6,38},{7,39},{8,40},{9,... | collective-permute-start | bytes 983048 | tf_op jit(solution)/shard_map/ppermute | solution.py:38
  64.7 12.5 %all-to-all-start.3 = ((f32[16,40,128]{2,1,0:T(8,128)}), f32[16,40,128]{2,1,0:T(8,128)S(1)}, u32[]{:S(2)}, u32[]{:S(2)}) async-start(f32[16,40,128]{2,1,0:T(8,128)} %bitcast.2), calls=%async_computation.3 | async-start | bytes 655360 | tf_op jit(solution)/shard_map/all_to_all | solution.py:42
  77.9 11.5 %all-to-all-start.4 = ((f32[8,40,128]{2,1,0:T(8,128)}), f32[8,40,128]{2,1,0:T(8,128)S(1)}, u32[]{:S(2)}, u32[]{:S(2)}) async-start(f32[8,40,128]{2,1,0:T(8,128)} %broadcast_in_dim.10), calls=%async_computation.4 | async-start | bytes 327680 | tf_op jit(solution)/shard_map/all_to_all | solution.py:42
  90.1 11.4 %all-to-all-start.5 = ((f32[16,40,128]{2,1,0:T(8,128)}), f32[16,40,128]{2,1,0:T(8,128)S(1)}, u32[]{:S(2)}, u32[]{:S(2)}) async-start(f32[16,40,128]{2,1,0:T(8,128)} %broadcast_in_dim.11), calls=%async_computation.5 | async-start | bytes 655360 | tf_op jit(solution)/shard_map/all_to_all | solution.py:42
  101.5 9.0 %copy-start.3 = (f32[147,512]{1,0:T(8,128)S(1)}, f32[147,512]{1,0:T(8,128)}, u32[]{:S(2)}) copy-start(f32[147,512]{1,0:T(8,128)} %coeffs.1) | copy-start | bytes 903172
  101.5 9.0 %collective-permute-start.3 = (f32[640,128]{1,0:T(8,128)S(1)}, f32[640,128]{1,0:T(8,128)S(1)}, u32[]{:S(2)}, u32[]{:S(2)}) collective-permute-start(f32[640,128]{1,0:T(8,128)S(1)} %bitcast.7), channel_id=1, source_target_pairs={{0,32},{1,33},{2,34},{3,35},{4,36},{5,37},{6,38},{7,39},{8,40},{9,... | collective-permute-start | bytes 983048 | tf_op jit(solution)/shard_map/ppermute | solution.py:38
  108.8 1.7 %copy-start.5 = (s32[2]{0:T(128)S(1)}, s32[2]{0:T(128)}, u32[]{:S(2)}) copy-start(s32[2]{0:T(128)} %owners.3) | copy-start | bytes 28
  108.9 1.6 %copy-start.7 = (s32[2]{0:T(128)S(1)}, s32[2]{0:T(128)}, u32[]{:S(2)}) copy-start(s32[2]{0:T(128)} %offsets.3) | copy-start | bytes 28
  108.9 1.6 %collective-permute-start.4 = (f32[256,256]{1,0:T(8,128)S(1)}, f32[256,256]{1,0:T(8,128)S(1)}, u32[]{:S(2)}, u32[]{:S(2)}) collective-permute-start(f32[256,256]{1,0:T(8,128)S(1)} %sweep.7.my_inverse), channel_id=1, source_target_pairs={{0,32},{1,33},{2,34},{3,35},{4,36},{5,37},{6,38},{7,39},{8,40},{9,... | collective-permute-start | bytes 786440 | tf_op jit(solution)/shard_map/ppermute | solution.py:38

commit v2 on v1

--- a/solution.py
+++ b/solution.py
@@ -25,8 +25,11 @@
 def rings():
     ys, cores, zs, xs = range(4), range(2), range(8), range(4)
     at = lambda y, c, z, x: (y * 2 + c) * 32 + z * 4 + x
-    planes = [[at(y, c, z, x) for y, x in itertools.product(ys, xs)] for c, z in itertools.product(cores, zs)]
-    lines = [[at(y, c, z, x) for z in zs] for y, c, x in itertools.product(ys, cores, xs)]
+    turn = lambda seq, c: [(i + 2 * c) % 4 for i in seq]
+    planes = [
+        [at(y, c, z, x) for y, x in itertools.product(turn(ys, c), turn(xs, c))] for c, z in itertools.product(cores, zs)
+    ]
+    lines = [[at(y, c, z, x) for z in (0, 4, 2, 6, 1, 5, 3, 7)] for y, c, x in itertools.product(ys, cores, xs)]
     partners = [(at(y, c, z, x), at(y, 1 - c, z, x)) for y, c, z, x in itertools.product(ys, cores, zs, xs)]
     return planes, lines, partners
 
@@ -60,11 +63,12 @@
     return exchange(replicate(value, len(groups[0])), groups)
 
 
-def all_reduce(kept, sent):
+def all_reduce(kept, sent, beside=None):
+    first, second, third = (lambda carry: carry,) * 3 if beside is None else beside
     value = kept + swap(sent)
-    value = scatter_sum(value, PLANES)
-    value = all_sum(value, LINES)
-    return collect(value, PLANES)
+    value, carry = lax.optimization_barrier((scatter_sum(value, PLANES), first(())))
+    value, carry = lax.optimization_barrier((all_sum(value, LINES), second(carry)))
+    return lax.optimization_barrier((collect(value, PLANES), third(carry)))
 
 
 def dot(left, right, dims):
@@ -88,33 +92,33 @@
     return jnp.where(first, mine, other), jnp.where(first, other, mine)
 
 
-def stage_kernel(owners, offsets, points, kept, sent):
+def stage_kernel(places, points, kept, sent):
     here = lax.axis_index(AXES)
     features, width = points.shape
     for step, out in ((core(), kept), (1 - core(), sent)):
 
-        @pl.when(owners[step] == here)
+        @pl.when(places[0, step] == here)
         def _():
-            turned = pltpu.roll(points[...], lax.rem(width - offsets[step], width), axis=1)
+            turned = pltpu.roll(points[...], lax.rem(width - places[1, step], width), axis=1)
             out[:features, :] = turned[:, :LANES]
             out[features : 2 * features, :] = turned[:, LANES : 2 * LANES]
             out[2 * features :, :] = jnp.zeros((out.shape[0] - 2 * features, LANES), jnp.float32)
 
-        @pl.when(owners[step] != here)
+        @pl.when(places[0, step] != here)
         def _():
             out[...] = jnp.zeros(out.shape, jnp.float32)
 
 
-def stage(owners, offsets, points):
+def stage(places, points):
     half = jax.ShapeDtypeStruct((up(2 * points.shape[0], 128), LANES), jnp.float32)
     return pl.pallas_call(
         stage_kernel,
         out_shape=(half, half),
-        in_specs=[SMEM, SMEM, VMEM],
+        in_specs=[SMEM, VMEM],
         out_specs=(VMEM, VMEM),
         name="stage",
         compiler_params=params(),
-    )(owners, offsets, points)
+    )(places, points)
 
 
 def kernel_values(left, right):
@@ -124,44 +128,62 @@
     return jnp.exp((2.0 * dot(left, right, ((0,), (0,))) - down - along) * (1.0 / features))
 
 
-def tiles_kernel(mine, other, points, residual, tiles, kept, sent):
-    features, classes = points.shape[0], residual.shape[0]
+def block_of(pieces, features):
+    return jnp.concatenate([pieces[i * features : (i + 1) * features, :] for i in range(2)], axis=1)
+
+
+def tile_kernel(mine, points, residual, tile, grad):
+    tile[...] = kernel_values(block_of(mine, points.shape[0]), points[...])
+    grad[...] = dot(residual[...], tile[...], ((1,), (1,)))
+
+
+def make_tile(mine, points, residual):
+    return pl.pallas_call(
+        tile_kernel,
+        out_shape=(
+            jax.ShapeDtypeStruct((BLOCK, points.shape[1]), jnp.float32),
+            jax.ShapeDtypeStruct((residual.shape[0], BLOCK), jnp.float32),
+        ),
+        in_specs=[VMEM] * 3,
+        out_specs=(VMEM, VMEM),
+        name="tile",
+        compiler_params=params(),
+        cost_estimate=pl.CostEstimate(flops=SWEEP_FLOPS // 4, bytes_accessed=1 << 20, transcendentals=0),
+    )(mine, points, residual)
+
+
+def products_kernel(my_tile, my_grad, other, points, residual, other_tile, kept, sent):
+    classes = residual.shape[0]
     rows = up(classes, 8)
-    pieces = [half[i * features : (i + 1) * features, :] for half in in_order(mine[...], other[...]) for i in range(2)]
-    tiles[...] = kernel_values(jnp.concatenate(pieces, axis=1), points[...])
-    grads = dot(residual[...], tiles[...], ((1,), (1,)))
-    overlap = dot(tiles[:BLOCK, :], tiles[BLOCK:, :], ((1,), (1,)))
+    other_tile[...] = kernel_values(block_of(other, points.shape[0]), points[...])
     gap = jnp.zeros((rows - classes, LANES), jnp.float32)
-    halves = []
-    for step in range(2):
-        left, right = (grads[:, (2 * step + i) * LANES : (2 * step + i + 1) * LANES] for i in range(2))
-        end = jnp.zeros((kept.shape[0] - 2 * rows - BLOCK, LANES), jnp.float32)
-        halves.append((left, right, overlap[:, step * LANES : (step + 1) * LANES], end))
-    for out, own in ((kept, 0), (sent, 1)):
-        left, right, products, end = (in_order(a, b)[own] for a, b in zip(*halves))
-        out[:classes, :] = left
+    end = jnp.zeros((kept.shape[0] - 2 * rows - BLOCK, LANES), jnp.float32)
+    overlap = dot(*in_order(my_tile[...], other_tile[...]), ((1,), (1,)))
+    products = in_order(overlap[:, :LANES], overlap[:, LANES:])
+    grads = (my_grad[...], dot(residual[...], other_tile[...], ((1,), (1,))))
+    for i, (out, grad) in enumerate(zip((kept, sent), grads)):
+        out[:classes, :] = grad[:, :LANES]
         out[classes:rows, :] = gap
-        out[rows : rows + classes, :] = right
+        out[rows : rows + classes, :] = grad[:, LANES:]
         out[rows + classes : 2 * rows, :] = gap
-        out[2 * rows : 2 * rows + BLOCK, :] = products
+        out[2 * rows : 2 * rows + BLOCK, :] = products[i]
         out[2 * rows + BLOCK :, :] = end
 
 
-def make_tiles(mine, other, points, residual):
-    width, rows = points.shape[1], up(residual.shape[0], 8)
-    half = jax.ShapeDtypeStruct((up(2 * rows + BLOCK, 128), LANES), jnp.float32)
-    return pl.pallas_call(
-        tiles_kernel,
-        out_shape=(jax.ShapeDtypeStruct((2 * BLOCK, width), jnp.float32), half, half),
-        in_specs=[VMEM] * 4,
+def make_products(my_tile, my_grad, other, points, residual):
+    half = jax.ShapeDtypeStruct((up(2 * up(residual.shape[0], 8) + BLOCK, 128), LANES), jnp.float32)
+    return pl.pallas_call(
+        products_kernel,
+        out_shape=(jax.ShapeDtypeStruct(my_tile.shape, jnp.float32), half, half),
+        in_specs=[VMEM] * 5,
         out_specs=(VMEM,) * 3,
-        name="tiles",
-        compiler_params=params(),
-    )(mine, other, points, residual)
+        name="products",
+        compiler_params=params(),
+    )(my_tile, my_grad, other, points, residual)
 
 
 def gram_kernel(features, mine, gram):
-    block = jnp.concatenate([mine[i * features : (i + 1) * features, :] for i in range(2)], axis=1)
+    block = block_of(mine, features)
     diagonal = lax.broadcasted_iota(jnp.int32, gram.shape, 0) == lax.broadcasted_iota(jnp.int32, gram.shape, 1)
     gram[...] = kernel_values(block, block) + jnp.where(diagonal, ridge, 0.0)
 
@@ -257,7 +279,7 @@
 
 
 def finish_kernel(
-    owners, offsets, my_sums, other_sums, my_inverse, other_inverse, tiles, residual, coeffs, new_residual, new_coeffs
+    places, my_sums, other_sums, my_inverse, other_inverse, my_tile, other_tile, residual, coeffs, new_residual, new_coeffs
 ):
     here = lax.axis_index(AXES)
     classes, width = residual.shape
@@ -274,36 +296,43 @@
     delta0 = direction(grads[0], inverses[0])
     delta1 = direction(grads[1] - dot(delta0, overlap, ((1,), (0,))), inverses[1])
     deltas = [delta[:classes] for delta in (delta0, delta1)]
-    new_residual[...] = residual[...] - dot(jnp.concatenate(deltas, axis=1), tiles[...], ((1,), (0,)))
+    tiles = in_order(my_tile[...], other_tile[...])
+    after0 = residual[...] - dot(deltas[0], tiles[0], ((1,), (0,)))
+    new_residual[...] = after0 - dot(deltas[1], tiles[1], ((1,), (0,)))
     new_coeffs[...] = coeffs[...]
     for step in range(2):
 
-        @pl.when(owners[step] == here)
+        @pl.when(places[0, step] == here)
         def _():
             wide = jnp.concatenate([deltas[step], jnp.zeros((classes, width - BLOCK), jnp.float32)], axis=1)
-            new_coeffs[...] = new_coeffs[...] + pltpu.roll(wide, offsets[step], axis=1)
-
-
-def finish(owners, offsets, *arrays):
+            new_coeffs[...] = new_coeffs[...] + pltpu.roll(wide, places[1, step], axis=1)
+
+
+def finish(places, *arrays):
     residual, coeffs = arrays[-2:]
     return pl.pallas_call(
         finish_kernel,
         out_shape=(jax.ShapeDtypeStruct(residual.shape, jnp.float32), jax.ShapeDtypeStruct(coeffs.shape, jnp.float32)),
-        in_specs=[SMEM, SMEM] + [VMEM] * 7,
+        in_specs=[SMEM] + [VMEM] * 8,
         out_specs=(VMEM, VMEM),
         name="finish",
         compiler_params=params(),
-    )(owners, offsets, *arrays)
+    )(places, *arrays)
 
 
 def body(points, residual, coeffs, owners, offsets):
-    mine = all_reduce(*stage(owners, offsets, points))
-    tiles, kept, sent = make_tiles(mine, swap(mine), points, residual)
-    inverse = make_gram(mine, points.shape[0])
-    for at in range(0, BLOCK, 64):
-        inverse = sweep(inverse, at, at + 64)
-    sums = all_reduce(kept, sent)
-    return finish(owners, offsets, sums, swap(sums), inverse, swap(inverse), tiles, residual, coeffs)
+    places = jnp.stack([owners, offsets])
+    mine, _ = all_reduce(*stage(places, points))
+    other, (my_tile, my_grad) = lax.optimization_barrier((swap(mine), make_tile(mine, points, residual)))
+    other_tile, kept, sent = make_products(my_tile, my_grad, other, points, residual)
+    gram = make_gram(mine, points.shape[0])
+
+    def last(gram):
+        inverse = sweep(gram, 192, 256)
+        return inverse, swap(inverse)
+
+    sums, inverses = all_reduce(kept, sent, (lambda _: sweep(gram, 0, 128), lambda m: sweep(m, 128, 192), last))
+    return finish(places, sums, swap(sums), *inverses, my_tile, other_tile, residual, coeffs)
 
 
 def solution(mesh):

time: 114 us -> 105 us (0.921)
  waiting for transfers between devices: 19.6 us -> 9.08 us
  starting transfers between devices: 22.6 us -> 29.3 us
  blocking collectives: 44.1 us -> 39.2 us
    all_to_all x3, waiting for transfers between devices: 14.7 us -> 3.99 us  [exchange(): lax.all_to_all(value, AXES, 0, 0, tiled=True, axis_index_groups=groups)]
    all_to_all x3, starting transfers between devices: 10.6 us -> 17.5 us  [exchange(): lax.all_to_all(value, AXES, 0, 0, tiled=True, axis_index_groups=groups)]
    all_to_all x3, blocking collectives: 44.1 us -> 39.2 us  [exchange(): lax.all_to_all(value, AXES, 0, 0, tiled=True, axis_index_groups=groups)]
    unnamed x16 -> x12, local copies, waits for them, and re-layouts: 2.5 us -> 1.84 us
    pallas_call x2 -> x3, Pallas kernels: 4.36 us -> 4.95 us  [the longest x1 2.27 us: make_products(): pl.pallas_call(products_kernel, out_shape=(jax.ShapeDtypeStruct(my_tile.s...]
    pallas_call x4 -> x3, Pallas kernels: 13.4 us -> 13.6 us  [sweep(): pl.pallas_call(functools.partial(sweep_kernel, first, last, size), out_sh...]
  transfers between devices with their start and end apart: 8 -> 8, of which waited for: 7 -> 5; matrix products, arithmetic and copies ran while one was open for 0% -> 0% of each run, Pallas kernels for 12% -> 16%
where the time goes in v2:
time: 105 us
  blocking collectives  39.2 us (37%)
  starting transfers between devices  29.3 us (28%)
  Pallas kernels  22.2 us (21%)
  waiting for transfers between devices  9.08 us (9%)
  local copies, waits for them, and re-layouts  3.31 us (3%)
    all_to_all x3, blocking collectives, exchange(): lax.all_to_all(value, AXES, 0, 0, tiled=True, axis_index_groups=groups)  39.2 us
    all_to_all x3, starting transfers between devices, exchange(): lax.all_to_all(value, AXES, 0, 0, tiled=True, axis_index_groups=groups)  17.5 us
    pallas_call x3, Pallas kernels, sweep(): pl.pallas_call(functools.partial(sweep_kernel, first, last, size), out_sh...  13.6 us
    ppermute x5, starting transfers between devices, swap(): return lax.ppermute(value, AXES, PARTNERS)  11.8 us
    ppermute x5, waiting for transfers between devices, swap(): return lax.ppermute(value, AXES, PARTNERS)  5.09 us
    all_to_all x3, waiting for transfers between devices, exchange(): lax.all_to_all(value, AXES, 0, 0, tiled=True, axis_index_groups=groups)  3.99 us
    pallas_call x1, Pallas kernels, finish(): pl.pallas_call(finish_kernel, out_shape=(jax.ShapeDtypeStruct(residual.sh...  2.98 us
    pallas_call x1, Pallas kernels, make_products(): pl.pallas_call(products_kernel, out_shape=(jax.ShapeDtypeStruct(my_tile.s...  2.27 us
  transfers between devices with their start and end apart: 8, of which 5 were waited for; matrix products, arithmetic and copies ran while one was open for 0% of the time, Pallas kernels for 16%

profile of v2, /device:TPU:1, one launch (start us, length us, event | category | flops | bytes accessed | tf_op | source)
XLA Modules:
  0.0 104.8 jit_solution(10087208331875066568)
XLA Ops:
  0.6 0.0 copy-start.4
  0.6 0.0 copy-start.5
  0.6 0.6 copy-done.4
  1.3 0.0 copy-done.5
  1.3 0.0 copy-start
  1.3 1.2 %copy-done = f32[440,512]{1,0:T(8,128)S(1)} copy-done((f32[440,512]{1,0:T(8,128)S(1)}, f32[440,512]{1,0:T(8,128)}, u32[]{:S(2)}) %copy-start) | copy-done | bytes 901144
  2.5 0.6 stage.1
  3.1 3.3 %collective-permute-start = (f32[896,128]{1,0:T(8,128)S(1)}, f32[896,128]{1,0:T(8,128)S(1)}, u32[]{:S(2)}, u32[]{:S(2)}) collective-permute-start(f32[896,128]{1,0:T(8,128)S(1)} %get-tuple-element.20), channel_id=1, source_target_pairs={{0,32},{1,33},{2,34},{3,35},{4,36},{5,37},{6,38},{7,39},{8,40},{9,... | collective-permute-start | bytes 1376264 | tf_op jit(solution)/shard_map/ppermute | solution.py:41
  6.4 1.4 %collective-permute-done = f32[896,128]{1,0:T(8,128)S(1)} collective-permute-done((f32[896,128]{1,0:T(8,128)S(1)}, f32[896,128]{1,0:T(8,128)S(1)}, u32[]{:S(2)}, u32[]{:S(2)}) %collective-permute-start) | collective-permute-done | bytes 458784 | tf_op jit(solution)/shard_map/ppermute | solution.py:41
  7.9 11.3 %all_to_all.48 = f32[16,56,128]{2,1,0:T(8,128)S(1)} all-to-all(f32[16,56,128]{2,1,0:T(8,128)S(1)} %bitcast.11), channel_id=1, replica_groups={{0,1,2,3,64,65,66,67,128,129,130,131,192,193,194,195},{4,5,6,7,68,69,70..., dimensions={0} | all-to-all | bytes 917504 | tf_op jit(solution)/shard_map/all_to_all | solution.py:45
  19.2 14.9 %all_to_all.49 = f32[8,56,128]{2,1,0:T(8,128)S(1)} all-to-all(f32[8,56,128]{2,1,0:T(8,128)S(1)} %broadcast_in_dim.8), channel_id=1, replica_groups={{0,16,8,24,4,20,12,28},{1,17,9,25,5,21,13,29},{2,18,10,26,6,22,14,30},{..., dimensions={0} | all-to-all | bytes 458752 | tf_op jit(solution)/shard_map/all_to_all | solution.py:45
  34.2 0.0 copy-start.1
  34.2 0.0 copy-start.2
  34.3 13.0 %all_to_all.50 = f32[16,56,128]{2,1,0:T(8,128)S(1)} all-to-all(f32[16,56,128]{2,1,0:T(8,128)S(1)} %broadcast_in_dim.9), channel_id=1, replica_groups={{0,1,2,3,64,65,66,67,128,129,130,131,192,193,194,195},{4,5,6,7,68,69,70..., dimensions={0} | all-to-all | bytes 917504 | tf_op jit(solution)/shard_map/all_to_all | solution.py:45
  47.2 5.9 %collective-permute-start.1 = (f32[896,128]{1,0:T(8,128)S(1)}, f32[896,128]{1,0:T(8,128)S(1)}, u32[]{:S(2)}, u32[]{:S(2)}) collective-permute-start(f32[896,128]{1,0:T(8,128)S(1)} %bitcast.8), channel_id=1, source_target_pairs={{0,32},{1,33},{2,34},{3,35},{4,36},{5,37},{6,38},{7,39},{8,40},{9,... | collective-permute-start | bytes 1376264 | tf_op jit(solution)/shard_map/ppermute | solution.py:41
  53.2 0.0 copy-done.1
  53.2 0.0 copy-done.2
  53.2 2.0 %tile.1 = (f32[256,512]{1,0:T(8,128)S(1)}, f32[147,256]{1,0:T(8,128)S(1)}) custom-call(f32[896,128]{1,0:T(8,128)S(1)} %bitcast.9, f32[440,512]{1,0:T(8,128)S(1)} %copy-done.1, f32[147,512]{1,0:T(8,128)S(1)} %copy-done.2), custom_call_target="tpu_custom_call" | custom-call | flops 1000000000 | bytes 1048576 | tf_op jit(solution)/shard_map/tile/pallas_call | solution.py:141
  55.2 0.0 collective-permute-done.1.other
  55.2 2.3 %products.1 = (f32[256,512]{1,0:T(8,128)S(1)}, f32[640,128]{1,0:T(8,128)S(1)}, f32[640,128]{1,0:T(8,128)S(1)}) custom-call(f32[256,512]{1,0:T(8,128)S(1)} %get-tuple-element.23.my_tile, f32[147,256]{1,0:T(8,128)S(1)} %get-tuple-element.24.my_grad, f32[896,128]{1,0:T(8,128)S(1)} %collective-permute-done.1.other, f32[440,512]{1,0:T(8,128)S(1)} %copy-done.1, ...), custom_call_target="tpu_custom_call" | custom-call | tf_op jit(solution)/shard_map/products/pallas_call | solution.py:175
  57.5 0.1 collective-permute-start.2
  57.6 0.7 gram.1.source
  58.4 0.9 collective-permute-done.2
  59.2 0.8 add.7
  60.0 6.7 %all-to-all-start.3 = ((f32[16,40,128]{2,1,0:T(8,128)}), f32[16,40,128]{2,1,0:T(8,128)S(1)}, u32[]{:S(2)}, u32[]{:S(2)}) async-start(f32[16,40,128]{2,1,0:T(8,128)} %bitcast.4), calls=%async_computation.3 | async-start | bytes 655360 | tf_op jit(solution)/shard_map/all_to_all | solution.py:45
  66.7 6.9 %sweep.3.source = f32[256,256]{1,0:T(8,128)S(1)} custom-call(f32[256,256]{1,0:T(8,128)S(1)} %gram.1.source), custom_call_target="tpu_custom_call" | custom-call | flops 8000000000 | bytes 1048576 | tf_op jit(solution)/shard_map/sweep/pallas_call | solution.py:270
  73.5 0.0 all-to-all-done.3
  73.6 0.7 broadcast_in_dim.10
  74.2 4.2 %all-to-all-start.4 = ((f32[8,40,128]{2,1,0:T(8,128)}), f32[8,40,128]{2,1,0:T(8,128)S(1)}, u32[]{:S(2)}, u32[]{:S(2)}) async-start(f32[8,40,128]{2,1,0:T(8,128)} %broadcast_in_dim.10), calls=%async_computation.4 | async-start | bytes 327680 | tf_op jit(solution)/shard_map/all_to_all | solution.py:45
  78.4 3.3 %sweep.4.source = f32[256,256]{1,0:T(8,128)S(1)} custom-call(f32[256,256]{1,0:T(8,128)S(1)} %sweep.3.source), custom_call_target="tpu_custom_call" | custom-call | flops 4000000000 | bytes 1048576 | tf_op jit(solution)/shard_map/sweep/pallas_call | solution.py:270
  81.7 4.0 %all-to-all-done.4 = f32[8,40,128]{2,1,0:T(8,128)S(1)} async-done(((f32[8,40,128]{2,1,0:T(8,128)}), f32[8,40,128]{2,1,0:T(8,128)S(1)}, u32[]{:S(2)}, u32[]{:S(2)}) %all-to-all-start.4) | async-done | bytes 163872 | tf_op jit(solution)/shard_map/all_to_all | solution.py:45
  85.7 0.7 broadcast_in_dim.11
  86.5 6.7 %all-to-all-start.5 = ((f32[16,40,128]{2,1,0:T(8,128)}), f32[16,40,128]{2,1,0:T(8,128)S(1)}, u32[]{:S(2)}, u32[]{:S(2)}) async-start(f32[16,40,128]{2,1,0:T(8,128)} %broadcast_in_dim.11), calls=%async_computation.5 | async-start | bytes 655360 | tf_op jit(solution)/shard_map/all_to_all | solution.py:45
  93.1 0.0 copy-start.3
  93.1 3.4 %sweep.5.my_inverse = f32[256,256]{1,0:T(8,128)S(1)} custom-call(f32[256,256]{1,0:T(8,128)S(1)} %sweep.4.source), custom_call_target="tpu_custom_call" | custom-call | flops 4000000000 | bytes 1048576 | tf_op jit(solution)/shard_map/sweep/pallas_call | solution.py:270
  96.6 0.1 collective-permute-start.3
  96.7 1.5 %collective-permute-done.3.other_inverse = f32[256,256]{1,0:T(8,128)S(1)} collective-permute-done((f32[256,256]{1,0:T(8,128)S(1)}, f32[256,256]{1,0:T(8,128)S(1)}, u32[]{:S(2)}, u32[]{:S(2)}) %collective-permute-start.3) | collective-permute-done | bytes 262176 | tf_op jit(solution)/shard_map/ppermute | solution.py:41
  98.2 0.0 all-to-all-done.5
  98.2 2.4 %collective-permute-start.4 = (f32[640,128]{1,0:T(8,128)S(1)}, f32[640,128]{1,0:T(8,128)S(1)}, u32[]{:S(2)}, u32[]{:S(2)}) collective-permute-start(f32[640,128]{1,0:T(8,128)S(1)} %bitcast.6), channel_id=1, source_target_pairs={{0,32},{1,33},{2,34},{3,35},{4,36},{5,37},{6,38},{7,39},{8,40},{9,... | collective-permute-start | bytes 983048 | tf_op jit(solution)/shard_map/ppermute | solution.py:41
  100.6 1.3 %collective-permute-done.4.other_sums = f32[640,128]{1,0:T(8,128)S(1)} collective-permute-done((f32[640,128]{1,0:T(8,128)S(1)}, f32[640,128]{1,0:T(8,128)S(1)}, u32[]{:S(2)}, u32[]{:S(2)}) %collective-permute-start.4) | collective-permute-done | bytes 327712 | tf_op jit(solution)/shard_map/ppermute | solution.py:41
  101.9 0.0 copy-done.3
  101.9 3.0 %finish.1 = (f32[147,512]{1,0:T(8,128)}, f32[147,512]{1,0:T(8,128)}) custom-call(s32[2,2]{1,0:T(2,128)S(1)} %pad_add_fusion.places, f32[640,128]{1,0:T(8,128)S(1)} %bitcast.7, f32[640,128]{1,0:T(8,128)S(1)} %collective-permute-done.4.other_sums, f32[256,256]{1,0:T(8,128)S(1)} %sweep.5.my_inverse, f32[256,256]{1,0:T(8,128)S(1)} %collective-permute-done.3.other_inverse, ...), custom_call_target="tpu_custom_call" | custom-call | tf_op jit(solution)/shard_map/finish/pallas_call | solution.py:313
  (8 shorter events, 0.2 us)
Async XLA Ops:
  0.6 0.7 copy-start.4
  0.6 0.7 copy-start.5
  1.3 1.2 %copy-start = (f32[440,512]{1,0:T(8,128)S(1)}, f32[440,512]{1,0:T(8,128)}, u32[]{:S(2)}) copy-start(f32[440,512]{1,0:T(8,128)} %points.5) | copy-start | bytes 2703364
  3.1 4.7 %collective-permute-start = (f32[896,128]{1,0:T(8,128)S(1)}, f32[896,128]{1,0:T(8,128)S(1)}, u32[]{:S(2)}, u32[]{:S(2)}) collective-permute-start(f32[896,128]{1,0:T(8,128)S(1)} %get-tuple-element.20), channel_id=1, source_target_pairs={{0,32},{1,33},{2,34},{3,35},{4,36},{5,37},{6,38},{7,39},{8,40},{9,... | collective-permute-start | bytes 1376264 | tf_op jit(solution)/shard_map/ppermute | solution.py:41
  34.2 19.0 %copy-start.1 = (f32[440,512]{1,0:T(8,128)S(1)}, f32[440,512]{1,0:T(8,128)}, u32[]{:S(2)}) copy-start(f32[440,512]{1,0:T(8,128)} %points.5) | copy-start | bytes 2703364
  34.2 18.9 %copy-start.2 = (f32[147,512]{1,0:T(8,128)S(1)}, f32[147,512]{1,0:T(8,128)}, u32[]{:S(2)}) copy-start(f32[147,512]{1,0:T(8,128)} %residual.5) | copy-start | bytes 903172
  47.2 8.0 %collective-permute-start.1 = (f32[896,128]{1,0:T(8,128)S(1)}, f32[896,128]{1,0:T(8,128)S(1)}, u32[]{:S(2)}, u32[]{:S(2)}) collective-permute-start(f32[896,128]{1,0:T(8,128)S(1)} %bitcast.8), channel_id=1, source_target_pairs={{0,32},{1,33},{2,34},{3,35},{4,36},{5,37},{6,38},{7,39},{8,40},{9,... | collective-permute-start | bytes 1376264 | tf_op jit(solution)/shard_map/ppermute | solution.py:41
  57.5 1.7 %collective-permute-start.2 = (f32[640,128]{1,0:T(8,128)S(1)}, f32[640,128]{1,0:T(8,128)S(1)}, u32[]{:S(2)}, u32[]{:S(2)}) collective-permute-start(f32[640,128]{1,0:T(8,128)S(1)} %get-tuple-element.27), channel_id=1, source_target_pairs={{0,32},{1,33},{2,34},{3,35},{4,36},{5,37},{6,38},{7,39},{8,40},{9,... | collective-permute-start | bytes 983048 | tf_op jit(solution)/shard_map/ppermute | solution.py:41
  60.0 13.5 %all-to-all-start.3 = ((f32[16,40,128]{2,1,0:T(8,128)}), f32[16,40,128]{2,1,0:T(8,128)S(1)}, u32[]{:S(2)}, u32[]{:S(2)}) async-start(f32[16,40,128]{2,1,0:T(8,128)} %bitcast.4), calls=%async_computation.3 | async-start | bytes 655360 | tf_op jit(solution)/shard_map/all_to_all | solution.py:45
  74.2 11.5 %all-to-all-start.4 = ((f32[8,40,128]{2,1,0:T(8,128)}), f32[8,40,128]{2,1,0:T(8,128)S(1)}, u32[]{:S(2)}, u32[]{:S(2)}) async-start(f32[8,40,128]{2,1,0:T(8,128)} %broadcast_in_dim.10), calls=%async_computation.4 | async-start | bytes 327680 | tf_op jit(solution)/shard_map/all_to_all | solution.py:45
  86.5 11.7 %all-to-all-start.5 = ((f32[16,40,128]{2,1,0:T(8,128)}), f32[16,40,128]{2,1,0:T(8,128)S(1)}, u32[]{:S(2)}, u32[]{:S(2)}) async-start(f32[16,40,128]{2,1,0:T(8,128)} %broadcast_in_dim.11), calls=%async_computation.5 | async-start | bytes 655360 | tf_op jit(solution)/shard_map/all_to_all | solution.py:45
  93.1 8.7 %copy-start.3 = (f32[147,512]{1,0:T(8,128)S(1)}, f32[147,512]{1,0:T(8,128)}, u32[]{:S(2)}) copy-start(f32[147,512]{1,0:T(8,128)} %coeffs.1) | copy-start | bytes 903172
  96.6 1.6 %collective-permute-start.3 = (f32[256,256]{1,0:T(8,128)S(1)}, f32[256,256]{1,0:T(8,128)S(1)}, u32[]{:S(2)}, u32[]{:S(2)}) collective-permute-start(f32[256,256]{1,0:T(8,128)S(1)} %sweep.5.my_inverse), channel_id=1, source_target_pairs={{0,32},{1,33},{2,34},{3,35},{4,36},{5,37},{6,38},{7,39},{8,40},{9,... | collective-permute-start | bytes 786440 | tf_op jit(solution)/shard_map/ppermute | solution.py:41
  98.2 3.7 %collective-permute-start.4 = (f32[640,128]{1,0:T(8,128)S(1)}, f32[640,128]{1,0:T(8,128)S(1)}, u32[]{:S(2)}, u32[]{:S(2)}) collective-permute-start(f32[640,128]{1,0:T(8,128)S(1)} %bitcast.6), channel_id=1, source_target_pairs={{0,32},{1,33},{2,34},{3,35},{4,36},{5,37},{6,38},{7,39},{8,40},{9,... | collective-permute-start | bytes 983048 | tf_op jit(solution)/shard_map/ppermute | solution.py:41

commit v3 on v2

--- a/solution.py
+++ b/solution.py
@@ -25,11 +25,8 @@
 def rings():
     ys, cores, zs, xs = range(4), range(2), range(8), range(4)
     at = lambda y, c, z, x: (y * 2 + c) * 32 + z * 4 + x
-    turn = lambda seq, c: [(i + 2 * c) % 4 for i in seq]
-    planes = [
-        [at(y, c, z, x) for y, x in itertools.product(turn(ys, c), turn(xs, c))] for c, z in itertools.product(cores, zs)
-    ]
-    lines = [[at(y, c, z, x) for z in (0, 4, 2, 6, 1, 5, 3, 7)] for y, c, x in itertools.product(ys, cores, xs)]
+    planes = [[at(y, c, z, x) for y, x in itertools.product((2, 3, 0, 1), repeat=2)] for c, z in itertools.product(cores, zs)]
+    lines = [[at(y, c, z, x) for z in (7, 3, 5, 1, 6, 2, 4, 0)] for y, c, x in itertools.product(ys, cores, xs)]
     partners = [(at(y, c, z, x), at(y, 1 - c, z, x)) for y, c, z, x in itertools.product(ys, cores, zs, xs)]
     return planes, lines, partners
 
@@ -75,6 +72,17 @@
     return lax.dot_general(left, right, (dims, ((), ())), precision=lax.Precision.HIGHEST, preferred_element_type=jnp.float32)
 
 
+def halves(value):
+    high = value.astype(jnp.bfloat16)
+    return high, (value - high.astype(jnp.float32)).astype(jnp.bfloat16)
+
+
+def dot_3(left, right, dims):
+    (left, left_rest), (right, right_rest) = halves(left), halves(right)
+    product = lambda a, b: lax.dot_general(a, b, (dims, ((), ())), preferred_element_type=jnp.float32)
+    return product(left, right_rest) + product(left_rest, right) + product(left, right)
+
+
 def up(count, to):
     return -(-count // to) * to
 
@@ -134,7 +142,7 @@
 
 def tile_kernel(mine, points, residual, tile, grad):
     tile[...] = kernel_values(block_of(mine, points.shape[0]), points[...])
-    grad[...] = dot(residual[...], tile[...], ((1,), (1,)))
+    grad[...] = dot_3(residual[...], tile[...], ((1,), (1,)))
 
 
 def make_tile(mine, points, residual):
@@ -158,9 +166,9 @@
     other_tile[...] = kernel_values(block_of(other, points.shape[0]), points[...])
     gap = jnp.zeros((rows - classes, LANES), jnp.float32)
     end = jnp.zeros((kept.shape[0] - 2 * rows - BLOCK, LANES), jnp.float32)
-    overlap = dot(*in_order(my_tile[...], other_tile[...]), ((1,), (1,)))
+    overlap = dot_3(*in_order(my_tile[...], other_tile[...]), ((1,), (1,)))
     products = in_order(overlap[:, :LANES], overlap[:, LANES:])
-    grads = (my_grad[...], dot(residual[...], other_tile[...], ((1,), (1,))))
+    grads = (my_grad[...], dot_3(residual[...], other_tile[...], ((1,), (1,))))
     for i, (out, grad) in enumerate(zip((kept, sent), grads)):
         out[:classes, :] = grad[:, :LANES]
         out[classes:rows, :] = gap
@@ -291,14 +299,14 @@
 
     def direction(grad, inverse):
         scale = step_norm / jnp.sqrt(jnp.sum(grad * grad) * (1.0 / (classes * BLOCK)) + 1e-06)
-        return dot(grad, inverse, ((1,), (0,))) * -scale
+        return dot_3(grad, inverse, ((1,), (0,))) * -scale
 
     delta0 = direction(grads[0], inverses[0])
-    delta1 = direction(grads[1] - dot(delta0, overlap, ((1,), (0,))), inverses[1])
+    delta1 = direction(grads[1] - dot_3(delta0, overlap, ((1,), (0,))), inverses[1])
     deltas = [delta[:classes] for delta in (delta0, delta1)]
     tiles = in_order(my_tile[...], other_tile[...])
-    after0 = residual[...] - dot(deltas[0], tiles[0], ((1,), (0,)))
-    new_residual[...] = after0 - dot(deltas[1], tiles[1], ((1,), (0,)))
+    after0 = residual[...] - dot_3(deltas[0], tiles[0], ((1,), (0,)))
+    new_residual[...] = after0 - dot_3(deltas[1], tiles[1], ((1,), (0,)))
     new_coeffs[...] = coeffs[...]
     for step in range(2):
 

time: 105 us -> 101 us (0.962)
  waiting for transfers between devices: 9.08 us -> 6.22 us
  blocking collectives: 39.2 us -> 37.8 us
  starting transfers between devices: 29.3 us -> 30.6 us
  Pallas kernels: 22.2 us -> 21 us
    all_to_all x3, starting transfers between devices: 17.5 us -> 20 us  [exchange(): lax.all_to_all(value, AXES, 0, 0, tiled=True, axis_index_groups=groups)]
    all_to_all x3, waiting for transfers between devices: 3.99 us -> 1.61 us  [exchange(): lax.all_to_all(value, AXES, 0, 0, tiled=True, axis_index_groups=groups)]
    all_to_all x3, blocking collectives: 39.2 us -> 37.8 us  [exchange(): lax.all_to_all(value, AXES, 0, 0, tiled=True, axis_index_groups=groups)]
    ppermute x5, starting transfers between devices: 11.8 us -> 10.6 us  [swap(): return lax.ppermute(value, AXES, PARTNERS)]
where the time goes in v3:
time: 101 us
  blocking collectives  37.8 us (37%)
  starting transfers between devices  30.6 us (30%)
  Pallas kernels  21 us (21%)
  waiting for transfers between devices  6.22 us (6%)
  local copies, waits for them, and re-layouts  3.31 us (3%)
    all_to_all x3, blocking collectives, exchange(): lax.all_to_all(value, AXES, 0, 0, tiled=True, axis_index_groups=groups)  37.8 us
    all_to_all x3, starting transfers between devices, exchange(): lax.all_to_all(value, AXES, 0, 0, tiled=True, axis_index_groups=groups)  20 us
    pallas_call x3, Pallas kernels, sweep(): pl.pallas_call(functools.partial(sweep_kernel, first, last, size), out_sh...  13.6 us
    ppermute x5, starting transfers between devices, swap(): return lax.ppermute(value, AXES, PARTNERS)  10.6 us
    ppermute x5, waiting for transfers between devices, swap(): return lax.ppermute(value, AXES, PARTNERS)  4.61 us
    pallas_call x1, Pallas kernels, finish(): pl.pallas_call(finish_kernel, out_shape=(jax.ShapeDtypeStruct(residual.sh...  2.58 us
  transfers between devices with their start and end apart: 8, of which 5 were waited for; matrix products, arithmetic and copies ran while one was open for 0% of the time, Pallas kernels for 16%

profile of v3, /device:TPU:1, one launch (start us, length us, event | category | flops | bytes accessed | tf_op | source)
XLA Modules:
  0.0 100.5 jit_solution(6945576784644891038)
XLA Ops:
  0.6 0.0 copy-start.4
  0.6 0.0 copy-start.5
  0.6 0.6 copy-done.4
  1.3 0.0 copy-done.5
  1.3 0.0 copy-start
  1.3 1.2 %copy-done = f32[440,512]{1,0:T(8,128)S(1)} copy-done((f32[440,512]{1,0:T(8,128)S(1)}, f32[440,512]{1,0:T(8,128)}, u32[]{:S(2)}) %copy-start) | copy-done | bytes 901144
  2.5 0.6 stage.1
  3.1 3.3 %collective-permute-start = (f32[896,128]{1,0:T(8,128)S(1)}, f32[896,128]{1,0:T(8,128)S(1)}, u32[]{:S(2)}, u32[]{:S(2)}) collective-permute-start(f32[896,128]{1,0:T(8,128)S(1)} %get-tuple-element.20), channel_id=1, source_target_pairs={{0,32},{1,33},{2,34},{3,35},{4,36},{5,37},{6,38},{7,39},{8,40},{9,... | collective-permute-start | bytes 1376264 | tf_op jit(solution)/shard_map/ppermute | solution.py:38
  6.4 1.4 %collective-permute-done = f32[896,128]{1,0:T(8,128)S(1)} collective-permute-done((f32[896,128]{1,0:T(8,128)S(1)}, f32[896,128]{1,0:T(8,128)S(1)}, u32[]{:S(2)}, u32[]{:S(2)}) %collective-permute-start) | collective-permute-done | bytes 458784 | tf_op jit(solution)/shard_map/ppermute | solution.py:38
  7.9 13.0 %all_to_all.48 = f32[16,56,128]{2,1,0:T(8,128)S(1)} all-to-all(f32[16,56,128]{2,1,0:T(8,128)S(1)} %bitcast.11), channel_id=1, replica_groups={{130,131,128,129,194,195,192,193,2,3,0,1,66,67,64,65},{134,135,132,133,..., dimensions={0} | all-to-all | bytes 917504 | tf_op jit(solution)/shard_map/all_to_all | solution.py:42
  21.0 13.8 %all_to_all.49 = f32[8,56,128]{2,1,0:T(8,128)S(1)} all-to-all(f32[8,56,128]{2,1,0:T(8,128)S(1)} %broadcast_in_dim.8), channel_id=1, replica_groups={{28,12,20,4,24,8,16,0},{29,13,21,5,25,9,17,1},{30,14,22,6,26,10,18,2},{..., dimensions={0} | all-to-all | bytes 458752 | tf_op jit(solution)/shard_map/all_to_all | solution.py:42
  34.8 0.0 copy-start.1
  34.9 0.0 copy-start.2
  34.9 11.0 %all_to_all.50 = f32[16,56,128]{2,1,0:T(8,128)S(1)} all-to-all(f32[16,56,128]{2,1,0:T(8,128)S(1)} %broadcast_in_dim.9), channel_id=1, replica_groups={{130,131,128,129,194,195,192,193,2,3,0,1,66,67,64,65},{134,135,132,133,..., dimensions={0} | all-to-all | bytes 917504 | tf_op jit(solution)/shard_map/all_to_all | solution.py:42
  45.8 3.9 %collective-permute-start.1 = (f32[896,128]{1,0:T(8,128)S(1)}, f32[896,128]{1,0:T(8,128)S(1)}, u32[]{:S(2)}, u32[]{:S(2)}) collective-permute-start(f32[896,128]{1,0:T(8,128)S(1)} %bitcast.8), channel_id=1, source_target_pairs={{0,32},{1,33},{2,34},{3,35},{4,36},{5,37},{6,38},{7,39},{8,40},{9,... | collective-permute-start | bytes 1376264 | tf_op jit(solution)/shard_map/ppermute | solution.py:38
  49.7 0.0 copy-done.1
  49.7 0.0 copy-done.2
  49.7 1.7 %tile.1 = (f32[256,512]{1,0:T(8,128)S(1)}, f32[147,256]{1,0:T(8,128)S(1)}) custom-call(f32[896,128]{1,0:T(8,128)S(1)} %bitcast.9, f32[440,512]{1,0:T(8,128)S(1)} %copy-done.1, f32[147,512]{1,0:T(8,128)S(1)} %copy-done.2), custom_call_target="tpu_custom_call" | custom-call | flops 1000000000 | bytes 1048576 | tf_op jit(solution)/shard_map/tile/pallas_call | solution.py:149
  51.4 0.0 collective-permute-done.1.other
  51.4 1.8 %products.1 = (f32[256,512]{1,0:T(8,128)S(1)}, f32[640,128]{1,0:T(8,128)S(1)}, f32[640,128]{1,0:T(8,128)S(1)}) custom-call(f32[256,512]{1,0:T(8,128)S(1)} %get-tuple-element.23.my_tile, f32[147,256]{1,0:T(8,128)S(1)} %get-tuple-element.24.my_grad, f32[896,128]{1,0:T(8,128)S(1)} %collective-permute-done.1.other, f32[440,512]{1,0:T(8,128)S(1)} %copy-done.1, ...), custom_call_target="tpu_custom_call" | custom-call | tf_op jit(solution)/shard_map/products/pallas_call | solution.py:183
  53.1 0.2 collective-permute-start.2
  53.4 0.7 gram.1.source
  54.1 0.7 collective-permute-done.2
  54.9 0.8 add.7
  55.6 7.0 %all-to-all-start.3 = ((f32[16,40,128]{2,1,0:T(8,128)}), f32[16,40,128]{2,1,0:T(8,128)S(1)}, u32[]{:S(2)}, u32[]{:S(2)}) async-start(f32[16,40,128]{2,1,0:T(8,128)} %bitcast.4), calls=%async_computation.3 | async-start | bytes 655360 | tf_op jit(solution)/shard_map/all_to_all | solution.py:42
  62.6 6.9 %sweep.3.source = f32[256,256]{1,0:T(8,128)S(1)} custom-call(f32[256,256]{1,0:T(8,128)S(1)} %gram.1.source), custom_call_target="tpu_custom_call" | custom-call | flops 8000000000 | bytes 1048576 | tf_op jit(solution)/shard_map/sweep/pallas_call | solution.py:278
  69.5 0.0 all-to-all-done.3
  69.5 0.7 broadcast_in_dim.10
  70.2 6.3 %all-to-all-start.4 = ((f32[8,40,128]{2,1,0:T(8,128)}), f32[8,40,128]{2,1,0:T(8,128)S(1)}, u32[]{:S(2)}, u32[]{:S(2)}) async-start(f32[8,40,128]{2,1,0:T(8,128)} %broadcast_in_dim.10), calls=%async_computation.4 | async-start | bytes 327680 | tf_op jit(solution)/shard_map/all_to_all | solution.py:42
  76.5 3.3 %sweep.4.source = f32[256,256]{1,0:T(8,128)S(1)} custom-call(f32[256,256]{1,0:T(8,128)S(1)} %sweep.3.source), custom_call_target="tpu_custom_call" | custom-call | flops 4000000000 | bytes 1048576 | tf_op jit(solution)/shard_map/sweep/pallas_call | solution.py:278
  79.8 1.6 %all-to-all-done.4 = f32[8,40,128]{2,1,0:T(8,128)S(1)} async-done(((f32[8,40,128]{2,1,0:T(8,128)}), f32[8,40,128]{2,1,0:T(8,128)S(1)}, u32[]{:S(2)}, u32[]{:S(2)}) %all-to-all-start.4) | async-done | bytes 163872 | tf_op jit(solution)/shard_map/all_to_all | solution.py:42
  81.4 0.7 broadcast_in_dim.11
  82.2 6.7 %all-to-all-start.5 = ((f32[16,40,128]{2,1,0:T(8,128)}), f32[16,40,128]{2,1,0:T(8,128)S(1)}, u32[]{:S(2)}, u32[]{:S(2)}) async-start(f32[16,40,128]{2,1,0:T(8,128)} %broadcast_in_dim.11), calls=%async_computation.5 | async-start | bytes 655360 | tf_op jit(solution)/shard_map/all_to_all | solution.py:42
  88.9 0.0 copy-start.3
  88.9 3.4 %sweep.5.my_inverse = f32[256,256]{1,0:T(8,128)S(1)} custom-call(f32[256,256]{1,0:T(8,128)S(1)} %sweep.4.source), custom_call_target="tpu_custom_call" | custom-call | flops 4000000000 | bytes 1048576 | tf_op jit(solution)/shard_map/sweep/pallas_call | solution.py:278
  92.3 2.8 %collective-permute-start.3 = (f32[256,256]{1,0:T(8,128)S(1)}, f32[256,256]{1,0:T(8,128)S(1)}, u32[]{:S(2)}, u32[]{:S(2)}) collective-permute-start(f32[256,256]{1,0:T(8,128)S(1)} %sweep.5.my_inverse), channel_id=1, source_target_pairs={{0,32},{1,33},{2,34},{3,35},{4,36},{5,37},{6,38},{7,39},{8,40},{9,... | collective-permute-start | bytes 786440 | tf_op jit(solution)/shard_map/ppermute | solution.py:38
  95.1 1.2 %collective-permute-done.3.other_inverse = f32[256,256]{1,0:T(8,128)S(1)} collective-permute-done((f32[256,256]{1,0:T(8,128)S(1)}, f32[256,256]{1,0:T(8,128)S(1)}, u32[]{:S(2)}, u32[]{:S(2)}) %collective-permute-start.3) | collective-permute-done | bytes 262176 | tf_op jit(solution)/shard_map/ppermute | solution.py:38
  96.3 0.0 all-to-all-done.5
  96.3 0.4 collective-permute-start.4
  96.7 1.3 %collective-permute-done.4.other_sums = f32[640,128]{1,0:T(8,128)S(1)} collective-permute-done((f32[640,128]{1,0:T(8,128)S(1)}, f32[640,128]{1,0:T(8,128)S(1)}, u32[]{:S(2)}, u32[]{:S(2)}) %collective-permute-start.4) | collective-permute-done | bytes 327712 | tf_op jit(solution)/shard_map/ppermute | solution.py:38
  97.9 0.0 copy-done.3
  97.9 2.6 %finish.1 = (f32[147,512]{1,0:T(8,128)}, f32[147,512]{1,0:T(8,128)}) custom-call(s32[2,2]{1,0:T(2,128)S(1)} %pad_add_fusion.places, f32[640,128]{1,0:T(8,128)S(1)} %bitcast.7, f32[640,128]{1,0:T(8,128)S(1)} %collective-permute-done.4.other_sums, f32[256,256]{1,0:T(8,128)S(1)} %sweep.5.my_inverse, f32[256,256]{1,0:T(8,128)S(1)} %collective-permute-done.3.other_inverse, ...), custom_call_target="tpu_custom_call" | custom-call | tf_op jit(solution)/shard_map/finish/pallas_call | solution.py:321
  (8 shorter events, 0.2 us)
Async XLA Ops:
  0.6 0.7 copy-start.4
  0.6 0.7 copy-start.5
  1.3 1.2 %copy-start = (f32[440,512]{1,0:T(8,128)S(1)}, f32[440,512]{1,0:T(8,128)}, u32[]{:S(2)}) copy-start(f32[440,512]{1,0:T(8,128)} %points.5) | copy-start | bytes 2703364
  3.1 4.7 %collective-permute-start = (f32[896,128]{1,0:T(8,128)S(1)}, f32[896,128]{1,0:T(8,128)S(1)}, u32[]{:S(2)}, u32[]{:S(2)}) collective-permute-start(f32[896,128]{1,0:T(8,128)S(1)} %get-tuple-element.20), channel_id=1, source_target_pairs={{0,32},{1,33},{2,34},{3,35},{4,36},{5,37},{6,38},{7,39},{8,40},{9,... | collective-permute-start | bytes 1376264 | tf_op jit(solution)/shard_map/ppermute | solution.py:38
  34.8 14.9 %copy-start.1 = (f32[440,512]{1,0:T(8,128)S(1)}, f32[440,512]{1,0:T(8,128)}, u32[]{:S(2)}) copy-start(f32[440,512]{1,0:T(8,128)} %points.5) | copy-start | bytes 2703364
  34.9 14.8 %copy-start.2 = (f32[147,512]{1,0:T(8,128)S(1)}, f32[147,512]{1,0:T(8,128)}, u32[]{:S(2)}) copy-start(f32[147,512]{1,0:T(8,128)} %residual.5) | copy-start | bytes 903172
  45.8 5.5 %collective-permute-start.1 = (f32[896,128]{1,0:T(8,128)S(1)}, f32[896,128]{1,0:T(8,128)S(1)}, u32[]{:S(2)}, u32[]{:S(2)}) collective-permute-start(f32[896,128]{1,0:T(8,128)S(1)} %bitcast.8), channel_id=1, source_target_pairs={{0,32},{1,33},{2,34},{3,35},{4,36},{5,37},{6,38},{7,39},{8,40},{9,... | collective-permute-start | bytes 1376264 | tf_op jit(solution)/shard_map/ppermute | solution.py:38
  53.1 1.7 %collective-permute-start.2 = (f32[640,128]{1,0:T(8,128)S(1)}, f32[640,128]{1,0:T(8,128)S(1)}, u32[]{:S(2)}, u32[]{:S(2)}) collective-permute-start(f32[640,128]{1,0:T(8,128)S(1)} %get-tuple-element.27), channel_id=1, source_target_pairs={{0,32},{1,33},{2,34},{3,35},{4,36},{5,37},{6,38},{7,39},{8,40},{9,... | collective-permute-start | bytes 983048 | tf_op jit(solution)/shard_map/ppermute | solution.py:38
  55.6 13.8 %all-to-all-start.3 = ((f32[16,40,128]{2,1,0:T(8,128)}), f32[16,40,128]{2,1,0:T(8,128)S(1)}, u32[]{:S(2)}, u32[]{:S(2)}) async-start(f32[16,40,128]{2,1,0:T(8,128)} %bitcast.4), calls=%async_computation.3 | async-start | bytes 655360 | tf_op jit(solution)/shard_map/all_to_all | solution.py:42
  70.2 11.2 %all-to-all-start.4 = ((f32[8,40,128]{2,1,0:T(8,128)}), f32[8,40,128]{2,1,0:T(8,128)S(1)}, u32[]{:S(2)}, u32[]{:S(2)}) async-start(f32[8,40,128]{2,1,0:T(8,128)} %broadcast_in_dim.10), calls=%async_computation.4 | async-start | bytes 327680 | tf_op jit(solution)/shard_map/all_to_all | solution.py:42
  82.2 14.1 %all-to-all-start.5 = ((f32[16,40,128]{2,1,0:T(8,128)}), f32[16,40,128]{2,1,0:T(8,128)S(1)}, u32[]{:S(2)}, u32[]{:S(2)}) async-start(f32[16,40,128]{2,1,0:T(8,128)} %broadcast_in_dim.11), calls=%async_computation.5 | async-start | bytes 655360 | tf_op jit(solution)/shard_map/all_to_all | solution.py:42
  88.9 9.1 %copy-start.3 = (f32[147,512]{1,0:T(8,128)S(1)}, f32[147,512]{1,0:T(8,128)}, u32[]{:S(2)}) copy-start(f32[147,512]{1,0:T(8,128)} %coeffs.1) | copy-start | bytes 903172
  92.3 4.0 %collective-permute-start.3 = (f32[256,256]{1,0:T(8,128)S(1)}, f32[256,256]{1,0:T(8,128)S(1)}, u32[]{:S(2)}, u32[]{:S(2)}) collective-permute-start(f32[256,256]{1,0:T(8,128)S(1)} %sweep.5.my_inverse), channel_id=1, source_target_pairs={{0,32},{1,33},{2,34},{3,35},{4,36},{5,37},{6,38},{7,39},{8,40},{9,... | collective-permute-start | bytes 786440 | tf_op jit(solution)/shard_map/ppermute | solution.py:38
  96.3 1.6 %collective-permute-start.4 = (f32[640,128]{1,0:T(8,128)S(1)}, f32[640,128]{1,0:T(8,128)S(1)}, u32[]{:S(2)}, u32[]{:S(2)}) collective-permute-start(f32[640,128]{1,0:T(8,128)S(1)} %bitcast.6), channel_id=1, source_target_pairs={{0,32},{1,33},{2,34},{3,35},{4,36},{5,37},{6,38},{7,39},{8,40},{9,... | collective-permute-start | bytes 983048 | tf_op jit(solution)/shard_map/ppermute | solution.py:38

commit v4 on v3

--- a/solution.py
+++ b/solution.py
@@ -257,9 +257,9 @@
     return p
 
 
-def sweep_kernel(first, last, size, source, out):
+def sweep_kernel(spans, source, out):
     n = out.shape[1]
-    for at in range(first, last, size):
+    for at, size in spans:
         along = lax.broadcasted_iota(jnp.int32, (size, n), 1)
         past = (along >= at) & (along < at + size)
         rows = source[at : at + size, :]
@@ -274,15 +274,15 @@
         source = out
 
 
-def sweep(gram, first, last, size=64):
-    return pl.pallas_call(
-        functools.partial(sweep_kernel, first, last, size),
+def sweep(gram, *spans):
+    return pl.pallas_call(
+        functools.partial(sweep_kernel, spans),
         out_shape=jax.ShapeDtypeStruct(gram.shape, gram.dtype),
         in_specs=[VMEM],
         out_specs=VMEM,
         name="sweep",
         compiler_params=params(),
-        cost_estimate=pl.CostEstimate(flops=SWEEP_FLOPS * (last - first) // 64, bytes_accessed=1 << 20, transcendentals=0),
+        cost_estimate=pl.CostEstimate(flops=SWEEP_FLOPS * sum(size for _, size in spans) // 64, bytes_accessed=1 << 20, transcendentals=0),
     )(gram)
 
 
@@ -336,10 +336,10 @@
     gram = make_gram(mine, points.shape[0])
 
     def last(gram):
-        inverse = sweep(gram, 192, 256)
+        inverse = sweep(gram, (192, 64))
         return inverse, swap(inverse)
 
-    sums, inverses = all_reduce(kept, sent, (lambda _: sweep(gram, 0, 128), lambda m: sweep(m, 128, 192), last))
+    sums, inverses = all_reduce(kept, sent, (lambda _: sweep(gram, (0, 64), (64, 32)), lambda m: sweep(m, (96, 32), (128, 64)), last))
     return finish(places, sums, swap(sums), *inverses, my_tile, other_tile, residual, coeffs)
 
 

time: 101 us -> 99.9 us (0.989)
  waiting for transfers between devices: 6.22 us -> 4.62 us
    all_to_all x3, waiting for transfers between devices: 1.61 us -> 0.01 us  [exchange(): lax.all_to_all(value, AXES, 0, 0, tiled=True, axis_index_groups=groups)]
  transfers between devices with their start and end apart: 8 -> 8, of which waited for: 5 -> 4; matrix products, arithmetic and copies ran while one was open for 0% -> 0% of each run, Pallas kernels for 16% -> 17%
where the time goes in v4:
time: 99.9 us; the launch traced here: 99.3 us
  blocking collectives  37.8 us (38%)
  starting transfers between devices  30.2 us (30%)
  Pallas kernels  21.8 us (22%)
  waiting for transfers between devices  4.62 us (5%)
  local copies, waits for them, and re-layouts  3.31 us (3%)
    all_to_all x3, blocking collectives, exchange(): lax.all_to_all(value, AXES, 0, 0, tiled=True, axis_index_groups=groups)  37.8 us
    all_to_all x3, starting transfers between devices, exchange(): lax.all_to_all(value, AXES, 0, 0, tiled=True, axis_index_groups=groups)  20 us
    pallas_call x3, Pallas kernels, sweep(): pl.pallas_call(functools.partial(sweep_kernel, spans), out_shape=jax.Shap...  14.4 us
    ppermute x5, starting transfers between devices, swap(): return lax.ppermute(value, AXES, PARTNERS)  10.2 us
    ppermute x5, waiting for transfers between devices, swap(): return lax.ppermute(value, AXES, PARTNERS)  4.61 us
    pallas_call x1, Pallas kernels, finish(): pl.pallas_call(finish_kernel, out_shape=(jax.ShapeDtypeStruct(residual.sh...  2.58 us
  transfers between devices with their start and end apart: 8, of which 4 were waited for; matrix products, arithmetic and copies ran while one was open for 0% of the time, Pallas kernels for 17%

profile of v4, /device:TPU:1, one launch (start us, length us, event | category | flops | bytes accessed | tf_op | source)
XLA Modules:
  0.0 99.3 jit_solution(12367862818198059768)
XLA Ops:
  0.6 0.0 copy-start.4
  0.6 0.0 copy-start.5
  0.6 0.6 copy-done.4
  1.3 0.0 copy-done.5
  1.3 0.0 copy-start
  1.3 1.2 %copy-done = f32[440,512]{1,0:T(8,128)S(1)} copy-done((f32[440,512]{1,0:T(8,128)S(1)}, f32[440,512]{1,0:T(8,128)}, u32[]{:S(2)}) %copy-start) | copy-done | bytes 901144
  2.5 0.6 stage.1
  3.1 3.3 %collective-permute-start = (f32[896,128]{1,0:T(8,128)S(1)}, f32[896,128]{1,0:T(8,128)S(1)}, u32[]{:S(2)}, u32[]{:S(2)}) collective-permute-start(f32[896,128]{1,0:T(8,128)S(1)} %get-tuple-element.20), channel_id=1, source_target_pairs={{0,32},{1,33},{2,34},{3,35},{4,36},{5,37},{6,38},{7,39},{8,40},{9,... | collective-permute-start | bytes 1376264 | tf_op jit(solution)/shard_map/ppermute | solution.py:38
  6.4 1.4 %collective-permute-done = f32[896,128]{1,0:T(8,128)S(1)} collective-permute-done((f32[896,128]{1,0:T(8,128)S(1)}, f32[896,128]{1,0:T(8,128)S(1)}, u32[]{:S(2)}, u32[]{:S(2)}) %collective-permute-start) | collective-permute-done | bytes 458784 | tf_op jit(solution)/shard_map/ppermute | solution.py:38
  7.9 13.0 %all_to_all.48 = f32[16,56,128]{2,1,0:T(8,128)S(1)} all-to-all(f32[16,56,128]{2,1,0:T(8,128)S(1)} %bitcast.11), channel_id=1, replica_groups={{130,131,128,129,194,195,192,193,2,3,0,1,66,67,64,65},{134,135,132,133,..., dimensions={0} | all-to-all | bytes 917504 | tf_op jit(solution)/shard_map/all_to_all | solution.py:42
  21.0 13.8 %all_to_all.49 = f32[8,56,128]{2,1,0:T(8,128)S(1)} all-to-all(f32[8,56,128]{2,1,0:T(8,128)S(1)} %broadcast_in_dim.8), channel_id=1, replica_groups={{28,12,20,4,24,8,16,0},{29,13,21,5,25,9,17,1},{30,14,22,6,26,10,18,2},{..., dimensions={0} | all-to-all | bytes 458752 | tf_op jit(solution)/shard_map/all_to_all | solution.py:42
  34.8 0.0 copy-start.1
  34.9 0.0 copy-start.2
  34.9 11.0 %all_to_all.50 = f32[16,56,128]{2,1,0:T(8,128)S(1)} all-to-all(f32[16,56,128]{2,1,0:T(8,128)S(1)} %broadcast_in_dim.9), channel_id=1, replica_groups={{130,131,128,129,194,195,192,193,2,3,0,1,66,67,64,65},{134,135,132,133,..., dimensions={0} | all-to-all | bytes 917504 | tf_op jit(solution)/shard_map/all_to_all | solution.py:42
  45.8 3.9 %collective-permute-start.1 = (f32[896,128]{1,0:T(8,128)S(1)}, f32[896,128]{1,0:T(8,128)S(1)}, u32[]{:S(2)}, u32[]{:S(2)}) collective-permute-start(f32[896,128]{1,0:T(8,128)S(1)} %bitcast.8), channel_id=1, source_target_pairs={{0,32},{1,33},{2,34},{3,35},{4,36},{5,37},{6,38},{7,39},{8,40},{9,... | collective-permute-start | bytes 1376264 | tf_op jit(solution)/shard_map/ppermute | solution.py:38
  49.7 0.0 copy-done.1
  49.7 0.0 copy-done.2
  49.7 1.7 %tile.1 = (f32[256,512]{1,0:T(8,128)S(1)}, f32[147,256]{1,0:T(8,128)S(1)}) custom-call(f32[896,128]{1,0:T(8,128)S(1)} %bitcast.9, f32[440,512]{1,0:T(8,128)S(1)} %copy-done.1, f32[147,512]{1,0:T(8,128)S(1)} %copy-done.2), custom_call_target="tpu_custom_call" | custom-call | flops 1000000000 | bytes 1048576 | tf_op jit(solution)/shard_map/tile/pallas_call | solution.py:149
  51.4 0.0 collective-permute-done.1.other
  51.4 1.8 %products.1 = (f32[256,512]{1,0:T(8,128)S(1)}, f32[640,128]{1,0:T(8,128)S(1)}, f32[640,128]{1,0:T(8,128)S(1)}) custom-call(f32[256,512]{1,0:T(8,128)S(1)} %get-tuple-element.23.my_tile, f32[147,256]{1,0:T(8,128)S(1)} %get-tuple-element.24.my_grad, f32[896,128]{1,0:T(8,128)S(1)} %collective-permute-done.1.other, f32[440,512]{1,0:T(8,128)S(1)} %copy-done.1, ...), custom_call_target="tpu_custom_call" | custom-call | tf_op jit(solution)/shard_map/products/pallas_call | solution.py:183
  53.1 0.2 collective-permute-start.2
  53.4 0.7 gram.1.source
  54.1 0.7 collective-permute-done.2
  54.9 0.8 add.7
  55.6 7.0 %all-to-all-start.3 = ((f32[16,40,128]{2,1,0:T(8,128)}), f32[16,40,128]{2,1,0:T(8,128)S(1)}, u32[]{:S(2)}, u32[]{:S(2)}) async-start(f32[16,40,128]{2,1,0:T(8,128)} %bitcast.4), calls=%async_computation.3 | async-start | bytes 655360 | tf_op jit(solution)/shard_map/all_to_all | solution.py:42
  62.6 5.4 %sweep.3.source = f32[256,256]{1,0:T(8,128)S(1)} custom-call(f32[256,256]{1,0:T(8,128)S(1)} %gram.1.source), custom_call_target="tpu_custom_call" | custom-call | flops 6000000000 | bytes 1048576 | tf_op jit(solution)/shard_map/sweep/pallas_call | solution.py:278
  68.0 0.0 all-to-all-done.3
  68.0 0.7 broadcast_in_dim.10
  68.7 6.3 %all-to-all-start.4 = ((f32[8,40,128]{2,1,0:T(8,128)}), f32[8,40,128]{2,1,0:T(8,128)S(1)}, u32[]{:S(2)}, u32[]{:S(2)}) async-start(f32[8,40,128]{2,1,0:T(8,128)} %broadcast_in_dim.10), calls=%async_computation.4 | async-start | bytes 327680 | tf_op jit(solution)/shard_map/all_to_all | solution.py:42
  75.0 5.6 %sweep.4.source = f32[256,256]{1,0:T(8,128)S(1)} custom-call(f32[256,256]{1,0:T(8,128)S(1)} %sweep.3.source), custom_call_target="tpu_custom_call" | custom-call | flops 6000000000 | bytes 1048576 | tf_op jit(solution)/shard_map/sweep/pallas_call | solution.py:278
  80.6 0.0 all-to-all-done.4
  80.7 0.7 broadcast_in_dim.11
  81.4 6.7 %all-to-all-start.5 = ((f32[16,40,128]{2,1,0:T(8,128)}), f32[16,40,128]{2,1,0:T(8,128)S(1)}, u32[]{:S(2)}, u32[]{:S(2)}) async-start(f32[16,40,128]{2,1,0:T(8,128)} %broadcast_in_dim.11), calls=%async_computation.5 | async-start | bytes 655360 | tf_op jit(solution)/shard_map/all_to_all | solution.py:42
  88.1 0.0 copy-start.3
  88.1 3.4 %sweep.5.my_inverse = f32[256,256]{1,0:T(8,128)S(1)} custom-call(f32[256,256]{1,0:T(8,128)S(1)} %sweep.4.source), custom_call_target="tpu_custom_call" | custom-call | flops 4000000000 | bytes 1048576 | tf_op jit(solution)/shard_map/sweep/pallas_call | solution.py:278
  91.5 2.5 %collective-permute-start.3 = (f32[256,256]{1,0:T(8,128)S(1)}, f32[256,256]{1,0:T(8,128)S(1)}, u32[]{:S(2)}, u32[]{:S(2)}) collective-permute-start(f32[256,256]{1,0:T(8,128)S(1)} %sweep.5.my_inverse), channel_id=1, source_target_pairs={{0,32},{1,33},{2,34},{3,35},{4,36},{5,37},{6,38},{7,39},{8,40},{9,... | collective-permute-start | bytes 786440 | tf_op jit(solution)/shard_map/ppermute | solution.py:38
  94.0 1.2 %collective-permute-done.3.other_inverse = f32[256,256]{1,0:T(8,128)S(1)} collective-permute-done((f32[256,256]{1,0:T(8,128)S(1)}, f32[256,256]{1,0:T(8,128)S(1)}, u32[]{:S(2)}, u32[]{:S(2)}) %collective-permute-start.3) | collective-permute-done | bytes 262176 | tf_op jit(solution)/shard_map/ppermute | solution.py:38
  95.1 0.0 all-to-all-done.5
  95.1 0.4 collective-permute-start.4
  95.5 1.3 %collective-permute-done.4.other_sums = f32[640,128]{1,0:T(8,128)S(1)} collective-permute-done((f32[640,128]{1,0:T(8,128)S(1)}, f32[640,128]{1,0:T(8,128)S(1)}, u32[]{:S(2)}, u32[]{:S(2)}) %collective-permute-start.4) | collective-permute-done | bytes 327712 | tf_op jit(solution)/shard_map/ppermute | solution.py:38
  96.8 0.0 copy-done.3
  96.8 2.6 %finish.1 = (f32[147,512]{1,0:T(8,128)}, f32[147,512]{1,0:T(8,128)}) custom-call(s32[2,2]{1,0:T(2,128)S(1)} %pad_add_fusion.places, f32[640,128]{1,0:T(8,128)S(1)} %bitcast.7, f32[640,128]{1,0:T(8,128)S(1)} %collective-permute-done.4.other_sums, f32[256,256]{1,0:T(8,128)S(1)} %sweep.5.my_inverse, f32[256,256]{1,0:T(8,128)S(1)} %collective-permute-done.3.other_inverse, ...), custom_call_target="tpu_custom_call" | custom-call | tf_op jit(solution)/shard_map/finish/pallas_call | solution.py:321
  (8 shorter events, 0.2 us)
Async XLA Ops:
  0.6 0.7 copy-start.4
  0.6 0.7 copy-start.5
  1.3 1.2 %copy-start = (f32[440,512]{1,0:T(8,128)S(1)}, f32[440,512]{1,0:T(8,128)}, u32[]{:S(2)}) copy-start(f32[440,512]{1,0:T(8,128)} %points.5) | copy-start | bytes 2703364
  3.1 4.7 %collective-permute-start = (f32[896,128]{1,0:T(8,128)S(1)}, f32[896,128]{1,0:T(8,128)S(1)}, u32[]{:S(2)}, u32[]{:S(2)}) collective-permute-start(f32[896,128]{1,0:T(8,128)S(1)} %get-tuple-element.20), channel_id=1, source_target_pairs={{0,32},{1,33},{2,34},{3,35},{4,36},{5,37},{6,38},{7,39},{8,40},{9,... | collective-permute-start | bytes 1376264 | tf_op jit(solution)/shard_map/ppermute | solution.py:38
  34.8 14.9 %copy-start.1 = (f32[440,512]{1,0:T(8,128)S(1)}, f32[440,512]{1,0:T(8,128)}, u32[]{:S(2)}) copy-start(f32[440,512]{1,0:T(8,128)} %points.5) | copy-start | bytes 2703364
  34.9 14.8 %copy-start.2 = (f32[147,512]{1,0:T(8,128)S(1)}, f32[147,512]{1,0:T(8,128)}, u32[]{:S(2)}) copy-start(f32[147,512]{1,0:T(8,128)} %residual.5) | copy-start | bytes 903172
  45.8 5.5 %collective-permute-start.1 = (f32[896,128]{1,0:T(8,128)S(1)}, f32[896,128]{1,0:T(8,128)S(1)}, u32[]{:S(2)}, u32[]{:S(2)}) collective-permute-start(f32[896,128]{1,0:T(8,128)S(1)} %bitcast.8), channel_id=1, source_target_pairs={{0,32},{1,33},{2,34},{3,35},{4,36},{5,37},{6,38},{7,39},{8,40},{9,... | collective-permute-start | bytes 1376264 | tf_op jit(solution)/shard_map/ppermute | solution.py:38
  53.1 1.7 %collective-permute-start.2 = (f32[640,128]{1,0:T(8,128)S(1)}, f32[640,128]{1,0:T(8,128)S(1)}, u32[]{:S(2)}, u32[]{:S(2)}) collective-permute-start(f32[640,128]{1,0:T(8,128)S(1)} %get-tuple-element.27), channel_id=1, source_target_pairs={{0,32},{1,33},{2,34},{3,35},{4,36},{5,37},{6,38},{7,39},{8,40},{9,... | collective-permute-start | bytes 983048 | tf_op jit(solution)/shard_map/ppermute | solution.py:38
  55.6 12.4 %all-to-all-start.3 = ((f32[16,40,128]{2,1,0:T(8,128)}), f32[16,40,128]{2,1,0:T(8,128)S(1)}, u32[]{:S(2)}, u32[]{:S(2)}) async-start(f32[16,40,128]{2,1,0:T(8,128)} %bitcast.4), calls=%async_computation.3 | async-start | bytes 655360 | tf_op jit(solution)/shard_map/all_to_all | solution.py:42
  68.7 11.9 %all-to-all-start.4 = ((f32[8,40,128]{2,1,0:T(8,128)}), f32[8,40,128]{2,1,0:T(8,128)S(1)}, u32[]{:S(2)}, u32[]{:S(2)}) async-start(f32[8,40,128]{2,1,0:T(8,128)} %broadcast_in_dim.10), calls=%async_computation.4 | async-start | bytes 327680 | tf_op jit(solution)/shard_map/all_to_all | solution.py:42
  81.4 13.7 %all-to-all-start.5 = ((f32[16,40,128]{2,1,0:T(8,128)}), f32[16,40,128]{2,1,0:T(8,128)S(1)}, u32[]{:S(2)}, u32[]{:S(2)}) async-start(f32[16,40,128]{2,1,0:T(8,128)} %broadcast_in_dim.11), calls=%async_computation.5 | async-start | bytes 655360 | tf_op jit(solution)/shard_map/all_to_all | solution.py:42
  88.1 8.7 %copy-start.3 = (f32[147,512]{1,0:T(8,128)S(1)}, f32[147,512]{1,0:T(8,128)}, u32[]{:S(2)}) copy-start(f32[147,512]{1,0:T(8,128)} %coeffs.1) | copy-start | bytes 903172
  91.5 3.6 %collective-permute-start.3 = (f32[256,256]{1,0:T(8,128)S(1)}, f32[256,256]{1,0:T(8,128)S(1)}, u32[]{:S(2)}, u32[]{:S(2)}) collective-permute-start(f32[256,256]{1,0:T(8,128)S(1)} %sweep.5.my_inverse), channel_id=1, source_target_pairs={{0,32},{1,33},{2,34},{3,35},{4,36},{5,37},{6,38},{7,39},{8,40},{9,... | collective-permute-start | bytes 786440 | tf_op jit(solution)/shard_map/ppermute | solution.py:38
  95.1 1.6 %collective-permute-start.4 = (f32[640,128]{1,0:T(8,128)S(1)}, f32[640,128]{1,0:T(8,128)S(1)}, u32[]{:S(2)}, u32[]{:S(2)}) collective-permute-start(f32[640,128]{1,0:T(8,128)S(1)} %bitcast.6), channel_id=1, source_target_pairs={{0,32},{1,33},{2,34},{3,35},{4,36},{5,37},{6,38},{7,39},{8,40},{9,... | collective-permute-start | bytes 983048 | tf_op jit(solution)/shard_map/ppermute | solution.py:38

commit v5 on v4

--- a/solution.py
+++ b/solution.py
@@ -25,7 +25,7 @@
 def rings():
     ys, cores, zs, xs = range(4), range(2), range(8), range(4)
     at = lambda y, c, z, x: (y * 2 + c) * 32 + z * 4 + x
-    planes = [[at(y, c, z, x) for y, x in itertools.product((2, 3, 0, 1), repeat=2)] for c, z in itertools.product(cores, zs)]
+    planes = [[at(y, c, z, x) for y, x in itertools.product((3, 0, 1, 2), repeat=2)] for c, z in itertools.product(cores, zs)]
     lines = [[at(y, c, z, x) for z in (7, 3, 5, 1, 6, 2, 4, 0)] for y, c, x in itertools.product(ys, cores, xs)]
     partners = [(at(y, c, z, x), at(y, 1 - c, z, x)) for y, c, z, x in itertools.product(ys, cores, zs, xs)]
     return planes, lines, partners

time: 99.9 us -> 100 us (level)
    ppermute x5, starting transfers between devices: 10.2 us -> 12.6 us  [swap(): return lax.ppermute(value, AXES, PARTNERS)]
    all_to_all x3, starting transfers between devices: 20 us -> 18.4 us  [exchange(): lax.all_to_all(value, AXES, 0, 0, tiled=True, axis_index_groups=groups)]
where the time goes in v5:
time: 100 us; the launch traced here: 99.9 us
  blocking collectives  37.6 us (38%)
  starting transfers between devices  31 us (31%)
  Pallas kernels  21.8 us (22%)
  waiting for transfers between devices  4.62 us (5%)
  local copies, waits for them, and re-layouts  3.31 us (3%)
    all_to_all x3, blocking collectives, exchange(): lax.all_to_all(value, AXES, 0, 0, tiled=True, axis_index_groups=groups)  37.6 us
    all_to_all x3, starting transfers between devices, exchange(): lax.all_to_all(value, AXES, 0, 0, tiled=True, axis_index_groups=groups)  18.4 us
    pallas_call x3, Pallas kernels, sweep(): pl.pallas_call(functools.partial(sweep_kernel, spans), out_shape=jax.Shap...  14.4 us
    ppermute x5, starting transfers between devices, swap(): return lax.ppermute(value, AXES, PARTNERS)  12.6 us
    ppermute x5, waiting for transfers between devices, swap(): return lax.ppermute(value, AXES, PARTNERS)  4.61 us
    pallas_call x1, Pallas kernels, finish(): pl.pallas_call(finish_kernel, out_shape=(jax.ShapeDtypeStruct(residual.sh...  2.58 us
  transfers between devices with their start and end apart: 8, of which 4 were waited for; matrix products, arithmetic and copies ran while one was open for 0% of the time, Pallas kernels for 17%

profile of v5, /device:TPU:1, one launch (start us, length us, event | category | flops | bytes accessed | tf_op | source)
XLA Modules:
  0.0 99.9 jit_solution(10747079772759480209)
XLA Ops:
  0.6 0.0 copy-start.4
  0.6 0.0 copy-start.5
  0.6 0.6 copy-done.4
  1.3 0.0 copy-done.5
  1.3 0.0 copy-start
  1.3 1.2 %copy-done = f32[440,512]{1,0:T(8,128)S(1)} copy-done((f32[440,512]{1,0:T(8,128)S(1)}, f32[440,512]{1,0:T(8,128)}, u32[]{:S(2)}) %copy-start) | copy-done | bytes 901144
  2.5 0.6 stage.1
  3.1 3.3 %collective-permute-start = (f32[896,128]{1,0:T(8,128)S(1)}, f32[896,128]{1,0:T(8,128)S(1)}, u32[]{:S(2)}, u32[]{:S(2)}) collective-permute-start(f32[896,128]{1,0:T(8,128)S(1)} %get-tuple-element.20), channel_id=1, source_target_pairs={{0,32},{1,33},{2,34},{3,35},{4,36},{5,37},{6,38},{7,39},{8,40},{9,... | collective-permute-start | bytes 1376264 | tf_op jit(solution)/shard_map/ppermute | solution.py:38
  6.4 1.4 %collective-permute-done = f32[896,128]{1,0:T(8,128)S(1)} collective-permute-done((f32[896,128]{1,0:T(8,128)S(1)}, f32[896,128]{1,0:T(8,128)S(1)}, u32[]{:S(2)}, u32[]{:S(2)}) %collective-permute-start) | collective-permute-done | bytes 458784 | tf_op jit(solution)/shard_map/ppermute | solution.py:38
  7.9 12.5 %all_to_all.48 = f32[16,56,128]{2,1,0:T(8,128)S(1)} all-to-all(f32[16,56,128]{2,1,0:T(8,128)S(1)} %bitcast.11), channel_id=1, replica_groups={{195,192,193,194,3,0,1,2,67,64,65,66,131,128,129,130},{199,196,197,198,..., dimensions={0} | all-to-all | bytes 917504 | tf_op jit(solution)/shard_map/all_to_all | solution.py:42
  20.5 13.6 %all_to_all.49 = f32[8,56,128]{2,1,0:T(8,128)S(1)} all-to-all(f32[8,56,128]{2,1,0:T(8,128)S(1)} %broadcast_in_dim.8), channel_id=1, replica_groups={{28,12,20,4,24,8,16,0},{29,13,21,5,25,9,17,1},{30,14,22,6,26,10,18,2},{..., dimensions={0} | all-to-all | bytes 458752 | tf_op jit(solution)/shard_map/all_to_all | solution.py:42
  34.1 0.0 copy-start.1
  34.2 0.0 copy-start.2
  34.2 11.4 %all_to_all.50 = f32[16,56,128]{2,1,0:T(8,128)S(1)} all-to-all(f32[16,56,128]{2,1,0:T(8,128)S(1)} %broadcast_in_dim.9), channel_id=1, replica_groups={{195,192,193,194,3,0,1,2,67,64,65,66,131,128,129,130},{199,196,197,198,..., dimensions={0} | all-to-all | bytes 917504 | tf_op jit(solution)/shard_map/all_to_all | solution.py:42
  45.6 5.4 %collective-permute-start.1 = (f32[896,128]{1,0:T(8,128)S(1)}, f32[896,128]{1,0:T(8,128)S(1)}, u32[]{:S(2)}, u32[]{:S(2)}) collective-permute-start(f32[896,128]{1,0:T(8,128)S(1)} %bitcast.8), channel_id=1, source_target_pairs={{0,32},{1,33},{2,34},{3,35},{4,36},{5,37},{6,38},{7,39},{8,40},{9,... | collective-permute-start | bytes 1376264 | tf_op jit(solution)/shard_map/ppermute | solution.py:38
  51.1 0.0 copy-done.1
  51.1 0.0 copy-done.2
  51.1 1.7 %tile.1 = (f32[256,512]{1,0:T(8,128)S(1)}, f32[147,256]{1,0:T(8,128)S(1)}) custom-call(f32[896,128]{1,0:T(8,128)S(1)} %bitcast.9, f32[440,512]{1,0:T(8,128)S(1)} %copy-done.1, f32[147,512]{1,0:T(8,128)S(1)} %copy-done.2), custom_call_target="tpu_custom_call" | custom-call | flops 1000000000 | bytes 1048576 | tf_op jit(solution)/shard_map/tile/pallas_call | solution.py:149
  52.7 0.0 collective-permute-done.1.other
  52.7 1.8 %products.1 = (f32[256,512]{1,0:T(8,128)S(1)}, f32[640,128]{1,0:T(8,128)S(1)}, f32[640,128]{1,0:T(8,128)S(1)}) custom-call(f32[256,512]{1,0:T(8,128)S(1)} %get-tuple-element.23.my_tile, f32[147,256]{1,0:T(8,128)S(1)} %get-tuple-element.24.my_grad, f32[896,128]{1,0:T(8,128)S(1)} %collective-permute-done.1.other, f32[440,512]{1,0:T(8,128)S(1)} %copy-done.1, ...), custom_call_target="tpu_custom_call" | custom-call | tf_op jit(solution)/shard_map/products/pallas_call | solution.py:183
  54.5 0.2 collective-permute-start.2
  54.7 0.7 gram.1.source
  55.5 0.7 collective-permute-done.2
  56.2 0.8 add.7
  57.0 7.0 %all-to-all-start.3 = ((f32[16,40,128]{2,1,0:T(8,128)}), f32[16,40,128]{2,1,0:T(8,128)S(1)}, u32[]{:S(2)}, u32[]{:S(2)}) async-start(f32[16,40,128]{2,1,0:T(8,128)} %bitcast.4), calls=%async_computation.3 | async-start | bytes 655360 | tf_op jit(solution)/shard_map/all_to_all | solution.py:42
  64.0 5.4 %sweep.3.source = f32[256,256]{1,0:T(8,128)S(1)} custom-call(f32[256,256]{1,0:T(8,128)S(1)} %gram.1.source), custom_call_target="tpu_custom_call" | custom-call | flops 6000000000 | bytes 1048576 | tf_op jit(solution)/shard_map/sweep/pallas_call | solution.py:278
  69.3 0.0 all-to-all-done.3
  69.4 0.7 broadcast_in_dim.10
  70.1 4.7 %all-to-all-start.4 = ((f32[8,40,128]{2,1,0:T(8,128)}), f32[8,40,128]{2,1,0:T(8,128)S(1)}, u32[]{:S(2)}, u32[]{:S(2)}) async-start(f32[8,40,128]{2,1,0:T(8,128)} %broadcast_in_dim.10), calls=%async_computation.4 | async-start | bytes 327680 | tf_op jit(solution)/shard_map/all_to_all | solution.py:42
  74.8 5.6 %sweep.4.source = f32[256,256]{1,0:T(8,128)S(1)} custom-call(f32[256,256]{1,0:T(8,128)S(1)} %sweep.3.source), custom_call_target="tpu_custom_call" | custom-call | flops 6000000000 | bytes 1048576 | tf_op jit(solution)/shard_map/sweep/pallas_call | solution.py:278
  80.4 0.0 all-to-all-done.4
  80.4 0.7 broadcast_in_dim.11
  81.1 6.7 %all-to-all-start.5 = ((f32[16,40,128]{2,1,0:T(8,128)}), f32[16,40,128]{2,1,0:T(8,128)S(1)}, u32[]{:S(2)}, u32[]{:S(2)}) async-start(f32[16,40,128]{2,1,0:T(8,128)} %broadcast_in_dim.11), calls=%async_computation.5 | async-start | bytes 655360 | tf_op jit(solution)/shard_map/all_to_all | solution.py:42
  87.8 0.0 copy-start.3
  87.8 3.4 %sweep.5.my_inverse = f32[256,256]{1,0:T(8,128)S(1)} custom-call(f32[256,256]{1,0:T(8,128)S(1)} %sweep.4.source), custom_call_target="tpu_custom_call" | custom-call | flops 4000000000 | bytes 1048576 | tf_op jit(solution)/shard_map/sweep/pallas_call | solution.py:278
  91.3 3.3 %collective-permute-start.3 = (f32[256,256]{1,0:T(8,128)S(1)}, f32[256,256]{1,0:T(8,128)S(1)}, u32[]{:S(2)}, u32[]{:S(2)}) collective-permute-start(f32[256,256]{1,0:T(8,128)S(1)} %sweep.5.my_inverse), channel_id=1, source_target_pairs={{0,32},{1,33},{2,34},{3,35},{4,36},{5,37},{6,38},{7,39},{8,40},{9,... | collective-permute-start | bytes 786440 | tf_op jit(solution)/shard_map/ppermute | solution.py:38
  94.5 1.2 %collective-permute-done.3.other_inverse = f32[256,256]{1,0:T(8,128)S(1)} collective-permute-done((f32[256,256]{1,0:T(8,128)S(1)}, f32[256,256]{1,0:T(8,128)S(1)}, u32[]{:S(2)}, u32[]{:S(2)}) %collective-permute-start.3) | collective-permute-done | bytes 262176 | tf_op jit(solution)/shard_map/ppermute | solution.py:38
  95.7 0.0 all-to-all-done.5
  95.7 0.4 collective-permute-start.4
  96.1 1.3 %collective-permute-done.4.other_sums = f32[640,128]{1,0:T(8,128)S(1)} collective-permute-done((f32[640,128]{1,0:T(8,128)S(1)}, f32[640,128]{1,0:T(8,128)S(1)}, u32[]{:S(2)}, u32[]{:S(2)}) %collective-permute-start.4) | collective-permute-done | bytes 327712 | tf_op jit(solution)/shard_map/ppermute | solution.py:38
  97.3 0.0 copy-done.3
  97.3 2.6 %finish.1 = (f32[147,512]{1,0:T(8,128)}, f32[147,512]{1,0:T(8,128)}) custom-call(s32[2,2]{1,0:T(2,128)S(1)} %pad_add_fusion.places, f32[640,128]{1,0:T(8,128)S(1)} %bitcast.7, f32[640,128]{1,0:T(8,128)S(1)} %collective-permute-done.4.other_sums, f32[256,256]{1,0:T(8,128)S(1)} %sweep.5.my_inverse, f32[256,256]{1,0:T(8,128)S(1)} %collective-permute-done.3.other_inverse, ...), custom_call_target="tpu_custom_call" | custom-call | tf_op jit(solution)/shard_map/finish/pallas_call | solution.py:321
  (8 shorter events, 0.2 us)
Async XLA Ops:
  0.6 0.7 copy-start.4
  0.6 0.7 copy-start.5
  1.3 1.2 %copy-start = (f32[440,512]{1,0:T(8,128)S(1)}, f32[440,512]{1,0:T(8,128)}, u32[]{:S(2)}) copy-start(f32[440,512]{1,0:T(8,128)} %points.5) | copy-start | bytes 2703364
  3.1 4.7 %collective-permute-start = (f32[896,128]{1,0:T(8,128)S(1)}, f32[896,128]{1,0:T(8,128)S(1)}, u32[]{:S(2)}, u32[]{:S(2)}) collective-permute-start(f32[896,128]{1,0:T(8,128)S(1)} %get-tuple-element.20), channel_id=1, source_target_pairs={{0,32},{1,33},{2,34},{3,35},{4,36},{5,37},{6,38},{7,39},{8,40},{9,... | collective-permute-start | bytes 1376264 | tf_op jit(solution)/shard_map/ppermute | solution.py:38
  34.1 16.9 %copy-start.1 = (f32[440,512]{1,0:T(8,128)S(1)}, f32[440,512]{1,0:T(8,128)}, u32[]{:S(2)}) copy-start(f32[440,512]{1,0:T(8,128)} %points.5) | copy-start | bytes 2703364
  34.2 16.9 %copy-start.2 = (f32[147,512]{1,0:T(8,128)S(1)}, f32[147,512]{1,0:T(8,128)}, u32[]{:S(2)}) copy-start(f32[147,512]{1,0:T(8,128)} %residual.5) | copy-start | bytes 903172
  45.6 7.1 %collective-permute-start.1 = (f32[896,128]{1,0:T(8,128)S(1)}, f32[896,128]{1,0:T(8,128)S(1)}, u32[]{:S(2)}, u32[]{:S(2)}) collective-permute-start(f32[896,128]{1,0:T(8,128)S(1)} %bitcast.8), channel_id=1, source_target_pairs={{0,32},{1,33},{2,34},{3,35},{4,36},{5,37},{6,38},{7,39},{8,40},{9,... | collective-permute-start | bytes 1376264 | tf_op jit(solution)/shard_map/ppermute | solution.py:38
  54.5 1.7 %collective-permute-start.2 = (f32[640,128]{1,0:T(8,128)S(1)}, f32[640,128]{1,0:T(8,128)S(1)}, u32[]{:S(2)}, u32[]{:S(2)}) collective-permute-start(f32[640,128]{1,0:T(8,128)S(1)} %get-tuple-element.27), channel_id=1, source_target_pairs={{0,32},{1,33},{2,34},{3,35},{4,36},{5,37},{6,38},{7,39},{8,40},{9,... | collective-permute-start | bytes 983048 | tf_op jit(solution)/shard_map/ppermute | solution.py:38
  57.0 12.4 %all-to-all-start.3 = ((f32[16,40,128]{2,1,0:T(8,128)}), f32[16,40,128]{2,1,0:T(8,128)S(1)}, u32[]{:S(2)}, u32[]{:S(2)}) async-start(f32[16,40,128]{2,1,0:T(8,128)} %bitcast.4), calls=%async_computation.3 | async-start | bytes 655360 | tf_op jit(solution)/shard_map/all_to_all | solution.py:42
  70.1 10.3 %all-to-all-start.4 = ((f32[8,40,128]{2,1,0:T(8,128)}), f32[8,40,128]{2,1,0:T(8,128)S(1)}, u32[]{:S(2)}, u32[]{:S(2)}) async-start(f32[8,40,128]{2,1,0:T(8,128)} %broadcast_in_dim.10), calls=%async_computation.4 | async-start | bytes 327680 | tf_op jit(solution)/shard_map/all_to_all | solution.py:42
  81.1 14.6 %all-to-all-start.5 = ((f32[16,40,128]{2,1,0:T(8,128)}), f32[16,40,128]{2,1,0:T(8,128)S(1)}, u32[]{:S(2)}, u32[]{:S(2)}) async-start(f32[16,40,128]{2,1,0:T(8,128)} %broadcast_in_dim.11), calls=%async_computation.5 | async-start | bytes 655360 | tf_op jit(solution)/shard_map/all_to_all | solution.py:42
  87.8 9.5 %copy-start.3 = (f32[147,512]{1,0:T(8,128)S(1)}, f32[147,512]{1,0:T(8,128)}, u32[]{:S(2)}) copy-start(f32[147,512]{1,0:T(8,128)} %coeffs.1) | copy-start | bytes 903172
  91.3 4.4 %collective-permute-start.3 = (f32[256,256]{1,0:T(8,128)S(1)}, f32[256,256]{1,0:T(8,128)S(1)}, u32[]{:S(2)}, u32[]{:S(2)}) collective-permute-start(f32[256,256]{1,0:T(8,128)S(1)} %sweep.5.my_inverse), channel_id=1, source_target_pairs={{0,32},{1,33},{2,34},{3,35},{4,36},{5,37},{6,38},{7,39},{8,40},{9,... | collective-permute-start | bytes 786440 | tf_op jit(solution)/shard_map/ppermute | solution.py:38
  95.7 1.6 %collective-permute-start.4 = (f32[640,128]{1,0:T(8,128)S(1)}, f32[640,128]{1,0:T(8,128)S(1)}, u32[]{:S(2)}, u32[]{:S(2)}) collective-permute-start(f32[640,128]{1,0:T(8,128)S(1)} %bitcast.6), channel_id=1, source_target_pairs={{0,32},{1,33},{2,34},{3,35},{4,36},{5,37},{6,38},{7,39},{8,40},{9,... | collective-permute-start | bytes 983048 | tf_op jit(solution)/shard_map/ppermute | solution.py:38
